TPU v7x, 32 devices: a whole 2x2x4 slice. The times are simulated.
32 devices in a mesh: lat: 8 (over z, y), depth: 4 (over x, core).
Axes of the slice: x: 2, y: 2, z: 4, core: 2. Of those that a mesh axis runs over, the one named last changes fastest.
Arguments:
- grade_field: float32 [64, 128, 2048], P('depth', 'lat'), may hold values from 0 to 1
- amplitude: float32 [64, 128, 2048], P('depth', 'lat'), may hold values from -6 to 6
- tf_table: int32 [4, 128], replicated, may hold values from 0 to 65535
- brick_mask: int32 [8, 16, 8], P('depth', 'lat'), may hold values 0 or 1
Outputs:
- frame: float32 [4, 128, 2048], P(None, 'lat', 'depth')
All inputs are finite; a program needn't handle non-finite values. No bound on the sum of `brick_mask` on one device may be relied on, other than what follows from the above.
Results may differ from a plain program's by a relative error of at most 0.00073.
Values sent between devices are 32-bit elements; how exact they have to be, the bound alone decides.
No kernel may reach another device: no remote copies, remote signals or barrier semaphores. Data moves between devices by JAX's collectives and lax.ppermute only.
A program may use at most 128 MiB of HBM per device.

v0:
```python
import functools

import jax
import jax.numpy as jnp
from jax import lax
from jax.experimental import pallas as pl
from jax.experimental.pallas import tpu as pltpu
from jax.sharding import PartitionSpec as P

MZ = 8
MX = 8
MY = 256
LANES = 128
SUB = 8
TERMS = 9


def sublane(shape):
    return lax.broadcasted_iota(jnp.int32, shape, len(shape) - 2)


def rows_kernel(last_parity, lat_ref, grade_hbm, amp_hbm, *refs):
    out_ref, sems = refs[-2:]
    slices, rows = grade_hbm.shape[:2]
    span = slices // 4

    def copies(first, places):
        made = []
        for f, src in enumerate((grade_hbm, amp_hbm)):
            for q in range(4):
                here = src.at[pl.ds(span * q, span), pl.ds(first, 2), :]
                made.append(pltpu.make_async_copy(here, out_ref.at[f, :, pl.ds(places[q], 2), :], sems.at[f, q]))
        for copy in made:
            copy.start()
        for copy in made:
            copy.wait()

    last = lax.rem(lat_ref[0], 2) == last_parity

    @pl.when(last)
    def _():
        copies(rows - 2, (0, 6, 4, 2))

    @pl.when(jnp.logical_not(last))
    def _():
        copies(0, (6, 4, 2, 0))


def slices_kernel(depth_ref, grade_hbm, amp_hbm, after_ref, near_ref, far_ref, sems):
    del after_ref
    slices = grade_hbm.shape[0]
    odd = lax.rem(depth_ref[0], 2)
    made = []
    for f, src in enumerate((grade_hbm, amp_hbm)):
        for n, (dst, at) in enumerate(((near_ref, 1 - odd), (far_ref, odd))):
            made.append(pltpu.make_async_copy(src.at[pl.ds(at * (slices - 2), 2)], dst.at[f], sems.at[f, n]))
    for copy in made:
        copy.start()
    for copy in made:
        copy.wait()


def round_weight(w):
    return w.astype(jnp.bfloat16).astype(jnp.float32)


def stencil(m2, m1, p1, p2):
    return (m2 - p2) + 8.0 * (p1 - m1)


def fill_tables(scale, table_ref, low_ref, high_ref):
    bins = table_ref.shape[1]
    table = (table_ref[...].astype(jnp.float32) / 65535.0).astype(jnp.bfloat16).astype(jnp.float32)
    table = jnp.where(sublane(table.shape) == 3, table * scale, table)
    column = lax.broadcasted_iota(jnp.int32, table.shape, 1)
    following = jnp.where(column == bins - 1, 0.0, pltpu.roll(table, bins - 1, 1))
    for c in range(4):
        low_ref[c] = jnp.broadcast_to(table[c:c + 1, :], (SUB, bins))
        high_ref[c] = jnp.broadcast_to(following[c:c + 1, :], (SUB, bins))


class Field:
    def __init__(self, ref, slices, strips, s):
        self.ref, self.strips = ref, strips
        self.per_slice = ref.shape[0] // slices
        self.s = s

    def load(self, z, rt, ds=0, k=0):
        start = pl.multiple_of((self.s + ds) * SUB, SUB) + (z * self.per_slice + rt * self.strips * SUB + k)
        return self.ref[pl.ds(start, SUB), :]

    def columns(self, z, rt, mid, lane):
        left = jnp.where(self.s > 0, self.load(z, rt, -jnp.minimum(self.s, 1)), 0.0)
        right = jnp.where(self.s < self.strips - 1, self.load(z, rt, jnp.minimum(self.strips - 1 - self.s, 1)), 0.0)
        return stencil(
            pltpu.roll(jnp.where(lane >= LANES - 2, left, mid), 2, 1),
            pltpu.roll(jnp.where(lane >= LANES - 1, left, mid), 1, 1),
            pltpu.roll(jnp.where(lane < 1, right, mid), LANES - 1, 1),
            pltpu.roll(jnp.where(lane < 2, right, mid), LANES - 2, 1),
        )

    def rows(self, z, rt, mid, sub, roll):
        def shifted(k):
            if k > 0:
                inside = sub < SUB - k
                if rt == 0:
                    return jnp.where(inside, self.load(z, 0, 0, k), self.load(z, 1, 0, k - SUB))
                return jnp.where(inside, pltpu.roll(mid, SUB - k, 0) if roll else self.load(z, 1, 0, k), 0.0)
            inside = sub >= -k
            if rt == 1:
                return jnp.where(inside, self.load(z, 1, 0, k), self.load(z, 0, 0, SUB + k))
            return jnp.where(inside, pltpu.roll(mid, -k, 0) if roll else self.load(z, 0, 0, k), 0.0)

        return stencil(*(shifted(k) for k in (-2, -1, 1, 2)))


def classify(grade, bins, low_ref, high_ref):
    position = grade * (bins - 1.0)
    index = jnp.minimum(position.astype(jnp.int32), bins - 1)
    w_low = 1.0 - (position - index.astype(jnp.float32))
    w_high = round_weight(1.0 - w_low)
    w_low = round_weight(w_low)

    def gather(ref, c):
        return jnp.take_along_axis(ref[c], index, axis=1)

    return [w_low * gather(low_ref, c) + w_high * gather(high_ref, c) for c in range(4)]


def step(state, terms):
    red, green, blue, trans = state
    g_x, a_x, g_yz, a_yz, steep, *cls = terms
    edge = 1.0 - 12.0 * lax.rsqrt(a_x * a_x + a_yz)
    shade = 0.3 + steep * lax.rsqrt(g_x * g_x + g_yz)
    weight = trans * (cls[3] * edge)
    trans = trans - weight
    weight = weight * shade
    return (red + weight * cls[0], green + weight * cls[1], blue + weight * cls[2], trans)


def cell_terms(fields, z, rt, along, roll, bins, low_ref, high_ref):
    lane = lax.broadcasted_iota(jnp.int32, (SUB, LANES), 1)
    sub = sublane((SUB, LANES))
    parts = []
    for field, near in zip(fields, along):
        mid = field.load(z, rt)
        dy = field.columns(z, rt, mid, lane)
        dz = stencil(*near)
        parts.append((mid, field.rows(z, rt, mid, sub, roll), dy * dy + dz * dz, dz))
    (grade, g_x, g_yz, g_z), (_, a_x, a_yz, _) = parts
    cls = classify(grade, bins, low_ref, high_ref)
    return (g_x, a_x, g_yz + 36.0, a_yz + 144.0, 0.7 * jnp.abs(g_z), *cls)


KEPT_AT = ((0, 4), (6, 2))


def keep(kept_ref, zi, s, rt, zb, terms):
    rows = slice(0, 2) if rt == 0 else slice(SUB - 2, SUB)
    at = KEPT_AT[rt][zb]
    for n, term in enumerate(terms):
        kept_ref[zi, s, n, at:at + 2, :] = term[rows, :]


def middle_kernel(scale, slices, strips, mask_ref, grade_ref, amp_ref, table_ref, mid_ref, kept_ref, low_ref, high_ref):
    bins = table_ref.shape[1]
    fill_tables(scale, table_ref, low_ref, high_ref)
    per_block = MY // LANES
    zero = jnp.zeros((SUB, LANES), jnp.float32)

    def block(cb, carry):
        for rt in range(2):
            for j in range(per_block):
                s = cb * per_block + j
                for c in range(3):
                    mid_ref[rt, s, c] = zero
                mid_ref[rt, s, 3] = zero + 1.0
            for zb in range(2):
                @pl.when(mask_ref[zb, rt, cb] != 0)
                def _():
                    for j in range(per_block):
                        s = cb * per_block + j
                        fields = [Field(ref, slices, strips, s) for ref in (grade_ref, amp_ref)]
                        state = tuple(mid_ref[rt, s, c] for c in range(4))
                        for zi in range(2 - 2 * zb, MZ - 2 * zb):
                            z = zb * MZ + zi
                            along = [[field.load(z + k, rt) for k in (-2, -1, 1, 2)] for field in fields]
                            terms = cell_terms(fields, z, rt, along, False, bins, low_ref, high_ref)
                            keep(kept_ref, zi, s, rt, zb, terms)
                            state = step(state, terms)
                        for c in range(4):
                            mid_ref[rt, s, c] = state[c]
        return carry

    lax.fori_loop(0, strips // per_block, block, 0)


def ends_kernel(scale, pieces, slices, strips, mask_ref, depth_ref, grade_ref, amp_ref, near_ref, far_ref, table_ref,
                mid_ref, *rest):
    outs, (kept_ref, acc_ref, low_ref, high_ref) = rest[:2], rest[2:]
    bins = table_ref.shape[1]
    fill_tables(scale, table_ref, low_ref, high_ref)
    per_block = MY // LANES
    piece_strips = strips // pieces
    piece_blocks = piece_strips // per_block
    zero = jnp.zeros((SUB, LANES), jnp.float32)
    odd = jnp.broadcast_to(lax.rem(depth_ref[0], 2), (SUB, LANES)) == 1

    def block(cb, carry):
        owner = lax.bitwise_xor(cb // piece_blocks, depth_ref[0])
        for rt in range(2):
            for zb in range(2):
                if zb == 0:
                    for j in range(per_block):
                        for c in range(3):
                            acc_ref[j, c] = zero
                        acc_ref[j, 3] = zero + 1.0
                else:
                    for j in range(per_block):
                        s = cb * per_block + j
                        trans = acc_ref[j, 3]
                        for c in range(3):
                            acc_ref[j, c] = acc_ref[j, c] + trans * mid_ref[rt, s, c]
                        acc_ref[j, 3] = trans * mid_ref[rt, s, 3]

                @pl.when(mask_ref[zb, rt, cb] != 0)
                def _():
                    for j in range(per_block):
                        s = cb * per_block + j
                        fields = [Field(ref, slices, strips, s) for ref in (grade_ref, amp_ref)]
                        halos = [[Field(ref, 4, strips, s) for ref in (near_ref, far_ref)]] * 2
                        state = tuple(acc_ref[j, c] for c in range(4))
                        for zi in (0, 1) if zb == 0 else (MZ - 2, MZ - 1):
                            z = zb * MZ + zi
                            along = []
                            for f in range(2):
                                near, far = halos[f]

                                def at(z):
                                    if 0 <= z < slices:
                                        return fields[f].load(z, rt)
                                    k = 2 * f + z % slices % 2
                                    one, two = near.load(k, rt), far.load(k, rt)
                                    return jnp.where(odd, one, two) if z < 0 else jnp.where(odd, two, one)

                                along.append([at(z + k) for k in (-2, -1, 1, 2)])
                            terms = cell_terms(fields, z, rt, along, True, bins, low_ref, high_ref)
                            keep(kept_ref, zi if zb == 0 else zi - 4, s, rt, zb, terms)
                            state = step(state, terms)
                        for c in range(4):
                            acc_ref[j, c] = state[c]
            for k, out in enumerate(outs):
                @pl.when(lax.rem(owner, 2) == k)
                def _():
                    for c in range(4):
                        for j in range(per_block):
                            part = lax.rem(cb, piece_blocks) * MY + j * LANES
                            lanes = pl.ds(pl.multiple_of(part, LANES), LANES)
                            out[owner // 2, c, rt * SUB:(rt + 1) * SUB, lanes] = acc_ref[j, c]
        return carry

    lax.fori_loop(0, strips // per_block, block, 0)


def edge_kernel(pieces, first, mask_ref, depth_ref, lat_ref, kept_ref, ends_ref, pair_ref, cross_ref, *refs):
    out_ref = refs[-1]
    half = kept_ref.shape[0]
    strips = kept_ref.shape[1]
    sub = sublane((SUB, LANES))
    is_first = lax.rem((sub + 2) // 4, 2) == 0
    odd_lat = jnp.broadcast_to(lax.rem(lat_ref[0], 2), (SUB, LANES))
    from_pair = lax.rem(sub // 2, 2) != odd_lat
    piece_strips = strips // pieces
    packs = piece_strips // 2

    above = lax.rem(sub // 2, 2) == 0
    even_row = lax.rem(sub, 2) == 0

    def outside(raw, above):
        mate = jnp.where(even_row, pltpu.roll(raw, SUB - 1, 0), pltpu.roll(raw, 1, 0))
        mate = jnp.where(above == even_row, 8.0 * mate, 0.0)
        return jnp.where(above, raw - mate, mate - raw)

    def halo(f, zi, lanes):
        pair, cross = pair_ref[f, zi % 4, :, lanes], cross_ref[f, zi % 4, :, lanes]
        if zi < 4:
            return outside(jnp.where(from_pair, pair, cross), above)
        return outside(pltpu.roll(jnp.where(from_pair, cross, pair), 2, 0), above)

    def strip(s):
        lanes = pl.ds(pl.multiple_of(s * LANES, LANES), LANES)
        cb = s // (MY // LANES)
        full = [[jnp.broadcast_to(mask_ref[zb, rt, cb], (SUB, LANES)) for rt in range(2)] for zb in range(2)]
        live = jnp.where(
            sub < 4, jnp.where(sub < 2, full[0][0], full[1][1]), jnp.where(sub < 6, full[1][0], full[0][1])
        ) != 0
        zero = jnp.zeros((SUB, LANES), jnp.float32)
        total = [zero, zero, zero]
        trans = zero + 1.0
        for zi in range(half):
            terms = [kept_ref[zi, s, n] for n in range(TERMS)]
            if zi < 2:
                terms = [jnp.where(is_first, ends_ref[zi, s, n], term) for n, term in enumerate(terms)]
            if zi >= half - 2:
                terms = [jnp.where(is_first, term, ends_ref[zi - half + 4, s, n]) for n, term in enumerate(terms)]
            g_x, a_x, g_yz, a_yz, steep, red, green, blue, alpha = terms
            g_x = g_x + halo(0, zi, lanes)
            a_x = a_x + halo(1, zi, lanes)
            edge = 1.0 - 12.0 * lax.rsqrt(a_x * a_x + a_yz)
            shade = 0.3 + steep * lax.rsqrt(g_x * g_x + g_yz)
            weight = jnp.where(live, trans * (alpha * edge), 0.0)
            trans = trans - weight
            weight = weight * shade
            total = [t + jnp.where(live, weight * c, 0.0) for t, c in zip(total, (red, green, blue))]
        out = [t + trans * pltpu.roll(t, 4, 0) for t in total]
        return out + [trans * pltpu.roll(trans, 4, 0)]

    def piece(n, carry):
        p = lax.bitwise_xor(first + n, depth_ref[0])
        results = [strip(p * piece_strips + j) for j in range(piece_strips)]
        for j in range(packs):
            packed = [
                jnp.where(is_first, one, pltpu.roll(two, 4, 0)) for one, two in zip(results[j], results[j + packs])
            ]
            for c in range(4):
                out_ref[n, c, :, j * LANES:(j + 1) * LANES] = packed[c]
        return carry

    lax.fori_loop(0, pieces // 2, piece, 0)


def merge(mine, other, rank, level):
    ahead = jnp.broadcast_to(lax.rem(lax.shift_right_logical(rank, level), 2), mine[3].shape) == 0
    clear = jnp.where(ahead, mine[3], other[3])
    return [
        jnp.where(ahead, m, o) + clear * jnp.where(ahead, o, m) for m, o in zip(mine[:3], other[:3])
    ] + [mine[3] * other[3]]


def channels(ref):
    return [ref[c] for c in range(4)]


def merge_kernel(depth_ref, stay_ref, got_ref, own_ref, away_ref):
    for n, out_ref in enumerate((own_ref, away_ref)):
        for c, value in enumerate(merge(channels(stay_ref.at[n]), channels(got_ref.at[n]), depth_ref[0], 0)):
            out_ref[c] = value


def finish_kernel(depth_ref, own_ref, got_ref, home_ref, beside_ref, across_ref, corner_ref, out_ref):
    rows = out_ref.shape[1]
    rank = depth_ref[0]
    frame = merge(channels(own_ref), channels(got_ref), rank, 1)
    near = merge(channels(home_ref.at[0]), channels(beside_ref.at[1]), rank, 0)
    far = merge(channels(across_ref.at[0]), channels(corner_ref.at[1]), rank, 0)
    rim = merge(near, far, rank, 1)
    for c in range(4):
        inner, packed = frame[c], rim[c]
        if c == 3:
            inner, packed = 1.0 - inner, 1.0 - packed
        wide = jnp.concatenate([packed, pltpu.roll(packed, 4, 0)], axis=1)
        sub = sublane(wide.shape)
        out_ref[c, 0:SUB, :] = jnp.where(sub < 2, wide, inner[0:SUB, :])
        out_ref[c, rows - SUB:rows, :] = jnp.where(sub >= SUB - 2, wide, inner[rows - SUB:rows, :])


def swap_near(x, axis):
    return lax.ppermute(x, axis, [(i, i ^ 1) for i in range(lax.axis_size(axis))])


def swap_far(x, axis):
    size = lax.axis_size(axis)
    return lax.ppermute(x, axis, [(i, j) for k in range(1, size - 1, 2) for i, j in ((k, k + 1), (k + 1, k))])


def by_strips(array):
    rows, cols = array.shape[-2:]
    split = array.reshape(-1, rows // SUB, SUB, cols // LANES, LANES)
    return split.transpose(0, 1, 3, 2, 4).reshape(-1, LANES)


def local(grade_field, amplitude, tf_table, brick_mask):
    slices, rows, cols = grade_field.shape
    pieces = lax.axis_size("depth")
    assert (slices, rows, pieces) == (2 * MZ, 2 * MX, 4)
    depth_rank = lax.axis_index("depth").astype(jnp.int32).reshape(1)
    lat_rank = lax.axis_index("lat").astype(jnp.int32).reshape(1)
    f32 = jnp.float32
    vmem = pl.BlockSpec(memory_space=pltpu.VMEM)
    smem = pl.BlockSpec(memory_space=pltpu.SMEM)
    hbm = pl.BlockSpec(memory_space=pltpu.MemorySpace.HBM)
    lat_halo = jax.ShapeDtypeStruct((2, slices // 4, SUB, cols), f32)
    depth_halo = jax.ShapeDtypeStruct((2, 2, rows, cols), f32)
    hbm_only = pltpu.MemorySpace.HBM
    fields = (grade_field, amplitude)
    grade_field = pltpu.with_memory_space_constraint(grade_field, hbm_only)
    amplitude = pltpu.with_memory_space_constraint(amplitude, hbm_only)
    small = pltpu.CompilerParams(vmem_limit_bytes=4 << 20)
    after = pl.BlockSpec(memory_space=pl.ANY)

    def take_rows(last_parity, *earlier):
        return pl.pallas_call(
            functools.partial(rows_kernel, last_parity),
            out_shape=lat_halo,
            in_specs=[smem, hbm, hbm] + [after] * len(earlier),
            out_specs=vmem,
            scratch_shapes=[pltpu.SemaphoreType.DMA((2, 4))],
            compiler_params=small,
            name="take_rows",
        )(lat_rank, grade_field, amplitude, *earlier)

    pair = take_rows(0)
    near, far = pl.pallas_call(
        slices_kernel,
        out_shape=(depth_halo, depth_halo),
        in_specs=[smem, hbm, hbm, after],
        out_specs=[vmem, vmem],
        scratch_shapes=[pltpu.SemaphoreType.DMA((2, 2))],
        compiler_params=small,
        name="take_slices",
    )(depth_rank, grade_field, amplitude, pair)
    cross = take_rows(1, far)
    pair = swap_near(pair, "lat")
    cross = swap_far(cross, "lat")
    near = swap_near(near, "depth")
    far = swap_far(far, "depth")
    piece = jax.ShapeDtypeStruct((4, rows, cols // pieces), f32)
    half = jax.ShapeDtypeStruct((2, *piece.shape), f32)
    scale = 4.0 / (slices * pieces)
    strips = cols // LANES
    table = pltpu.VMEM((4, SUB, tf_table.shape[1]), f32)
    grade_strips, amp_strips = by_strips(fields[0]), by_strips(fields[1])
    mid, kept = pl.pallas_call(
        functools.partial(middle_kernel, scale, slices, strips),
        out_shape=(
            jax.ShapeDtypeStruct((2, strips, 4, SUB, LANES), f32),
            jax.ShapeDtypeStruct((MZ, strips, TERMS, SUB, LANES), f32),
        ),
        in_specs=[smem, vmem, vmem, vmem],
        out_specs=[vmem, vmem],
        scratch_shapes=[table, table],
        compiler_params=pltpu.CompilerParams(vmem_limit_bytes=8 << 20),
        cost_estimate=pl.CostEstimate(flops=10**10, bytes_accessed=10**8, transcendentals=0),
        name="middle",
    )(brick_mask, grade_strips, amp_strips, tf_table)
    stay, go, kept_ends = pl.pallas_call(
        functools.partial(ends_kernel, scale, pieces, slices, strips),
        out_shape=(half, half, jax.ShapeDtypeStruct((4, strips, TERMS, SUB, LANES), f32)),
        in_specs=[smem, smem] + [vmem] * 6,
        out_specs=[vmem] * 3,
        scratch_shapes=[pltpu.VMEM((MY // LANES, 4, SUB, LANES), f32), table, table],
        compiler_params=pltpu.CompilerParams(vmem_limit_bytes=8 << 20),
        name="ends",
    )(brick_mask, depth_rank, grade_strips, amp_strips, by_strips(near), by_strips(far), tf_table, mid)

    def swap_across(x):
        return lax.ppermute(x, "depth", [(i, i ^ 2) for i in range(pieces)])

    own, away_inner = pl.pallas_call(
        merge_kernel,
        out_shape=(piece, piece),
        in_specs=[smem, vmem, vmem],
        out_specs=[vmem, vmem],
        compiler_params=small,
        name="merge",
    )(depth_rank, stay, swap_near(go, "depth"))
    got = swap_across(away_inner)
    rims = jax.ShapeDtypeStruct((2, 4, SUB, cols // pieces // 2), f32)

    def edges_of(first, *earlier):
        return pl.pallas_call(
            functools.partial(edge_kernel, pieces, first),
            out_shape=rims,
            in_specs=[smem, smem, smem, vmem, vmem, vmem, vmem] + [after] * len(earlier),
            out_specs=vmem,
            compiler_params=small,
            name="edges",
        )(brick_mask, depth_rank, lat_rank, kept, kept_ends, pair, cross, *earlier)

    away = edges_of(2, away_inner)
    home = edges_of(0, away)
    across = swap_across(away)
    edges = (home, swap_near(home, "depth"), across, swap_near(across, "depth"))
    return pl.pallas_call(
        finish_kernel,
        out_shape=piece,
        in_specs=[smem] + [vmem] * 6,
        out_specs=vmem,
        compiler_params=small,
        name="finish",
    )(depth_rank, own, got, *edges)


def solution(mesh):
    placed = (P("depth", "lat", None), P("depth", "lat", None), P(), P("depth", "lat", None))
    return jax.shard_map(
        local, mesh=mesh, in_specs=placed, out_specs=P(None, "lat", "depth"), check_vma=False
    )
```

profile of v0, /device:TPU:21, one launch (start us, length us, event | category | flops | bytes accessed | tf_op | source)
XLA Modules:
  0.0 34.8 jit_solution(3957139463091476446)
XLA Ops:
  0.0 1.1 %take_rows.2.after_ref = f32[2,4,8,2048]{3,2,1,0:T(8,128)S(1)} custom-call(s32[1]{0:T(128)} %bitcast.7.lat_ref, f32[16,16,2048]{2,1,0:T(8,128)} %grade_hbm.5, f32[16,16,2048]{2,1,0:T(8,128)} %amp_hbm.5), custom_call_target="tpu_custom_call" | custom-call | tf_op jit(solution)/shard_map/take_rows/pallas_call | solution.py:402
  1.1 0.3 collective-permute-start.4
  1.4 1.2 %take_slices.1 = (f32[2,2,16,2048]{3,2,1,0:T(8,128)S(1)}, f32[2,2,16,2048]{3,2,1,0:T(8,128)S(1)}) custom-call(s32[1]{0:T(128)} %bitcast.depth_ref, f32[16,16,2048]{2,1,0:T(8,128)} %grade_hbm.5, f32[16,16,2048]{2,1,0:T(8,128)} %amp_hbm.5, f32[2,4,8,2048]{3,2,1,0:T(8,128)S(1)} %take_rows.2.after_ref), custom_call_target="tpu_custom_call" | custom-call | tf_op jit(solution)/shard_map/take_slices/pallas_call | solution.py:413
  2.7 0.0 copy-start
  2.7 0.0 copy-start.1
  2.7 0.0 copy-start.2
  2.7 0.0 copy-start.3
  2.7 4.2 %collective-permute-start.1 = (f32[2,2,16,2048]{3,2,1,0:T(8,128)S(1)}, f32[2,2,16,2048]{3,2,1,0:T(8,128)S(1)}, u32[]{:S(2)}, u32[]{:S(2)}) collective-permute-start(f32[2,2,16,2048]{3,2,1,0:T(8,128)S(1)} %get-tuple-element.15.refs_0_), channel_id=1, source_target_pairs={{1,2},{2,1},{5,6},{6,5},{9,10},{10,9},{13,14},{14,13},{17,18},{18,... | collective-permute-start | bytes 1572872 | tf_op jit(solution)/shard_map/ppermute | solution.py:373
  6.9 1.2 %take_rows.3 = f32[2,4,8,2048]{3,2,1,0:T(8,128)S(1)} custom-call(s32[1]{0:T(128)} %bitcast.7.lat_ref, f32[16,16,2048]{2,1,0:T(8,128)} %grade_hbm.5, f32[16,16,2048]{2,1,0:T(8,128)} %amp_hbm.5, f32[2,2,16,2048]{3,2,1,0:T(8,128)S(1)} %get-tuple-element.15.refs_0_), custom_call_target="tpu_custom_call" | custom-call | tf_op jit(solution)/shard_map/take_rows/pallas_call | solution.py:402
  8.1 4.2 %collective-permute-start.5 = (f32[2,4,8,2048]{3,2,1,0:T(8,128)S(1)}, f32[2,4,8,2048]{3,2,1,0:T(8,128)S(1)}, u32[]{:S(2)}, u32[]{:S(2)}) collective-permute-start(f32[2,4,8,2048]{3,2,1,0:T(8,128)S(1)} %take_rows.3), channel_id=1, source_target_pairs={{4,8},{8,4},{12,16},{16,12},{20,24},{24,20},{5,9},{9,5},{13,17},{1... | collective-permute-start | bytes 1572872 | tf_op jit(solution)/shard_map/ppermute | solution.py:373
  12.3 0.1 collective-permute-start
  12.4 0.0 copy-done
  12.4 0.0 copy-done.1
  12.4 0.0 copy-done.2
  12.4 0.0 copy-done.3
  12.4 5.9 %middle.1 = (f32[2,16,4,8,128]{4,3,2,1,0:T(8,128)S(1)}, f32[8,16,9,8,128]{4,3,2,1,0:T(8,128)S(1)}) custom-call(s32[2,2,8]{2,1,0:T(2,128)S(1)} %copy-done.2, f32[4096,128]{1,0:T(8,128)S(1)} %bitcast.22, f32[4096,128]{1,0:T(8,128)S(1)} %bitcast.24, s32[4,128]{1,0:T(4,128)S(1)} %copy-done.3), custom_call_target="tpu_custom_call" | custom-call | flops 10000000000 | bytes 100000000 | tf_op jit(solution)/shard_map/middle/pallas_call | solution.py:433
  18.4 0.0 collective-permute-done
  18.4 0.0 collective-permute-done.1
  18.4 3.7 %ends.1 = (f32[2,4,16,512]{3,2,1,0:T(8,128)S(1)}, f32[2,4,16,512]{3,2,1,0:T(8,128)S(1)}, f32[4,16,9,8,128]{4,3,2,1,0:T(8,128)S(1)}) custom-call(s32[2,2,8]{2,1,0:T(2,128)S(1)} %copy-done.2, s32[1]{0:T(128)} %bitcast.depth_ref, f32[4096,128]{1,0:T(8,128)S(1)} %bitcast.23, f32[4096,128]{1,0:T(8,128)S(1)} %bitcast.25, f32[1024,128]{1,0:T(8,128)S(1)} %bitcast.27, ...), custom_call_target="tpu_custom_call" | custom-call | tf_op jit(solution)/shard_map/ends/pallas_call | solution.py:446
  22.1 2.5 %collective-permute-start.2 = (f32[2,4,16,512]{3,2,1,0:T(8,128)S(1)}, f32[2,4,16,512]{3,2,1,0:T(8,128)S(1)}, u32[]{:S(2)}, u32[]{:S(2)}) collective-permute-start(f32[2,4,16,512]{3,2,1,0:T(8,128)S(1)} %get-tuple-element.18), channel_id=1, source_target_pairs={{0,1},{1,0},{2,3},{3,2},{4,5},{5,4},{6,7},{7,6},{8,9},{9,8},{10,11... | collective-permute-start | bytes 786440 | tf_op jit(solution)/shard_map/ppermute | solution.py:368
  24.6 1.2 %collective-permute-done.2.got_ref = f32[2,4,16,512]{3,2,1,0:T(8,128)S(1)} collective-permute-done((f32[2,4,16,512]{3,2,1,0:T(8,128)S(1)}, f32[2,4,16,512]{3,2,1,0:T(8,128)S(1)}, u32[]{:S(2)}, u32[]{:S(2)}) %collective-permute-start.2) | collective-permute-done | bytes 262176 | tf_op jit(solution)/shard_map/ppermute | solution.py:368
  25.8 0.1 collective-permute-start.3
  25.9 0.0 collective-permute-done.4.pair_ref
  25.9 0.0 collective-permute-done.5.cross_ref
  25.9 1.1 %edges.2.refs_0_ = f32[2,4,8,256]{3,2,1,0:T(8,128)S(1)} custom-call(s32[2,2,8]{2,1,0:T(2,128)S(1)} %copy-done.2, s32[1]{0:T(128)} %bitcast.depth_ref, s32[1]{0:T(128)} %bitcast.7.lat_ref, f32[8,16,9,8,128]{4,3,2,1,0:T(8,128)S(1)} %get-tuple-element.21.kept_ref, f32[4,16,9,8,128]{4,3,2,1,0:T(8,128)S(1)} %get-tuple-element.22.ends_ref, ...), custom_call_target="tpu_custom_call" | custom-call | tf_op jit(solution)/shard_map/edges/pallas_call | solution.py:471
  27.0 1.5 %collective-permute-start.7 = (f32[2,4,8,256]{3,2,1,0:T(8,128)S(1)}, f32[2,4,8,256]{3,2,1,0:T(8,128)S(1)}, u32[]{:S(2)}, u32[]{:S(2)}) collective-permute-start(f32[2,4,8,256]{3,2,1,0:T(8,128)S(1)} %edges.2.refs_0_), channel_id=1, source_target_pairs={{0,2},{1,3},{2,0},{3,1},{4,6},{5,7},{6,4},{7,5},{8,10},{9,11},{10,... | collective-permute-start | bytes 196616 | tf_op jit(solution)/shard_map/ppermute | solution.py:457
  28.5 1.1 %edges.3.home_ref = f32[2,4,8,256]{3,2,1,0:T(8,128)S(1)} custom-call(s32[2,2,8]{2,1,0:T(2,128)S(1)} %copy-done.2, s32[1]{0:T(128)} %bitcast.depth_ref, s32[1]{0:T(128)} %bitcast.7.lat_ref, f32[8,16,9,8,128]{4,3,2,1,0:T(8,128)S(1)} %get-tuple-element.21.kept_ref, f32[4,16,9,8,128]{4,3,2,1,0:T(8,128)S(1)} %get-tuple-element.22.ends_ref, ...), custom_call_target="tpu_custom_call" | custom-call | tf_op jit(solution)/shard_map/edges/pallas_call | solution.py:471
  29.6 1.0 %collective-permute-start.6 = (f32[2,4,8,256]{3,2,1,0:T(8,128)S(1)}, f32[2,4,8,256]{3,2,1,0:T(8,128)S(1)}, u32[]{:S(2)}, u32[]{:S(2)}) collective-permute-start(f32[2,4,8,256]{3,2,1,0:T(8,128)S(1)} %edges.3.home_ref), channel_id=1, source_target_pairs={{0,1},{1,0},{2,3},{3,2},{4,5},{5,4},{6,7},{7,6},{8,9},{9,8},{10,11... | collective-permute-start | bytes 196616 | tf_op jit(solution)/shard_map/ppermute | solution.py:368
  30.6 1.4 %collective-permute-done.7.across_ref = f32[2,4,8,256]{3,2,1,0:T(8,128)S(1)} collective-permute-done((f32[2,4,8,256]{3,2,1,0:T(8,128)S(1)}, f32[2,4,8,256]{3,2,1,0:T(8,128)S(1)}, u32[]{:S(2)}, u32[]{:S(2)}) %collective-permute-start.7) | collective-permute-done | bytes 65568 | tf_op jit(solution)/shard_map/ppermute | solution.py:457
  32.0 1.2 %collective-permute-start.8 = (f32[2,4,8,256]{3,2,1,0:T(8,128)S(1)}, f32[2,4,8,256]{3,2,1,0:T(8,128)S(1)}, u32[]{:S(2)}, u32[]{:S(2)}) collective-permute-start(f32[2,4,8,256]{3,2,1,0:T(8,128)S(1)} %collective-permute-done.7.across_ref), channel_id=1, source_target_pairs={{0,1},{1,0},{2,3},{3,2},{4,5},{5,4},{6,7},{7,6},{8,9},{9,8},{10,11... | collective-permute-start | bytes 196616 | tf_op jit(solution)/shard_map/ppermute | solution.py:368
  33.2 0.0 collective-permute-done.6.beside_ref
  33.2 0.0 collective-permute-done.3.got_ref
  33.2 0.9 %collective-permute-done.8.corner_ref = f32[2,4,8,256]{3,2,1,0:T(8,128)S(1)} collective-permute-done((f32[2,4,8,256]{3,2,1,0:T(8,128)S(1)}, f32[2,4,8,256]{3,2,1,0:T(8,128)S(1)}, u32[]{:S(2)}, u32[]{:S(2)}) %collective-permute-start.8) | collective-permute-done | bytes 65568 | tf_op jit(solution)/shard_map/ppermute | solution.py:368
  34.1 0.7 %finish.1 = f32[4,16,512]{2,1,0:T(8,128)} custom-call(s32[1]{0:T(128)} %bitcast.depth_ref, f32[4,16,512]{2,1,0:T(8,128)S(1)} %get-tuple-element.19.own_ref, f32[4,16,512]{2,1,0:T(8,128)S(1)} %collective-permute-done.3.got_ref, f32[2,4,8,256]{3,2,1,0:T(8,128)S(1)} %edges.3.home_ref, f32[2,4,8,256]{3,2,1,0:T(8,128)S(1)} %collective-permute-done.6.beside_ref, ...), custom_call_target="tpu_custom_call" | custom-call | tf_op jit(solution)/shard_map/finish/pallas_call | solution.py:484
  (1 shorter events, 0.0 us)
Async XLA Ops:
  1.1 24.8 %collective-permute-start.4 = (f32[2,4,8,2048]{3,2,1,0:T(8,128)S(1)}, f32[2,4,8,2048]{3,2,1,0:T(8,128)S(1)}, u32[]{:S(2)}, u32[]{:S(2)}) collective-permute-start(f32[2,4,8,2048]{3,2,1,0:T(8,128)S(1)} %take_rows.2.after_ref), channel_id=1, source_target_pairs={{0,4},{4,0},{8,12},{12,8},{16,20},{20,16},{24,28},{28,24},{1,5},{5... | collective-permute-start | bytes 1572872 | tf_op jit(solution)/shard_map/ppermute | solution.py:368
  2.7 9.7 %copy-start = (f32[16,16,2048]{2,1,0:T(8,128)S(1)}, f32[16,16,2048]{2,1,0:T(8,128)}, u32[]{:S(2)}) copy-start(f32[16,16,2048]{2,1,0:T(8,128)} %grade_hbm.5) | copy-start | bytes 6291460
  2.7 9.7 %copy-start.1 = (f32[16,16,2048]{2,1,0:T(8,128)S(1)}, f32[16,16,2048]{2,1,0:T(8,128)}, u32[]{:S(2)}) copy-start(f32[16,16,2048]{2,1,0:T(8,128)} %amp_hbm.5) | copy-start | bytes 6291460
  2.7 9.7 %copy-start.2 = (s32[2,2,8]{2,1,0:T(2,128)S(1)}, s32[2,2,8]{2,1,0:T(2,128)}, u32[]{:S(2)}) copy-start(s32[2,2,8]{2,1,0:T(2,128)} %mask_ref.7) | copy-start | bytes 388
  2.7 9.7 %copy-start.3 = (s32[4,128]{1,0:T(4,128)S(1)}, s32[4,128]{1,0:T(4,128)}, u32[]{:S(2)}) copy-start(s32[4,128]{1,0:T(4,128)} %table_ref.3) | copy-start | bytes 6148
  2.7 15.7 %collective-permute-start.1 = (f32[2,2,16,2048]{3,2,1,0:T(8,128)S(1)}, f32[2,2,16,2048]{3,2,1,0:T(8,128)S(1)}, u32[]{:S(2)}, u32[]{:S(2)}) collective-permute-start(f32[2,2,16,2048]{3,2,1,0:T(8,128)S(1)} %get-tuple-element.15.refs_0_), channel_id=1, source_target_pairs={{1,2},{2,1},{5,6},{6,5},{9,10},{10,9},{13,14},{14,13},{17,18},{18,... | collective-permute-start | bytes 1572872 | tf_op jit(solution)/shard_map/ppermute | solution.py:373
  8.1 17.8 %collective-permute-start.5 = (f32[2,4,8,2048]{3,2,1,0:T(8,128)S(1)}, f32[2,4,8,2048]{3,2,1,0:T(8,128)S(1)}, u32[]{:S(2)}, u32[]{:S(2)}) collective-permute-start(f32[2,4,8,2048]{3,2,1,0:T(8,128)S(1)} %take_rows.3), channel_id=1, source_target_pairs={{4,8},{8,4},{12,16},{16,12},{20,24},{24,20},{5,9},{9,5},{13,17},{1... | collective-permute-start | bytes 1572872 | tf_op jit(solution)/shard_map/ppermute | solution.py:373
  12.3 6.1 %collective-permute-start = (f32[2,2,16,2048]{3,2,1,0:T(8,128)S(1)}, f32[2,2,16,2048]{3,2,1,0:T(8,128)S(1)}, u32[]{:S(2)}, u32[]{:S(2)}) collective-permute-start(f32[2,2,16,2048]{3,2,1,0:T(8,128)S(1)} %get-tuple-element.14), channel_id=1, source_target_pairs={{0,1},{1,0},{2,3},{3,2},{4,5},{5,4},{6,7},{7,6},{8,9},{9,8},{10,11... | collective-permute-start | bytes 1572872 | tf_op jit(solution)/shard_map/ppermute | solution.py:368
  22.1 3.7 %collective-permute-start.2 = (f32[2,4,16,512]{3,2,1,0:T(8,128)S(1)}, f32[2,4,16,512]{3,2,1,0:T(8,128)S(1)}, u32[]{:S(2)}, u32[]{:S(2)}) collective-permute-start(f32[2,4,16,512]{3,2,1,0:T(8,128)S(1)} %get-tuple-element.18), channel_id=1, source_target_pairs={{0,1},{1,0},{2,3},{3,2},{4,5},{5,4},{6,7},{7,6},{8,9},{9,8},{10,11... | collective-permute-start | bytes 786440 | tf_op jit(solution)/shard_map/ppermute | solution.py:368
  25.8 7.4 %collective-permute-start.3 = (f32[4,16,512]{2,1,0:T(8,128)S(1)}, f32[4,16,512]{2,1,0:T(8,128)S(1)}, u32[]{:S(2)}, u32[]{:S(2)}) collective-permute-start(f32[4,16,512]{2,1,0:T(8,128)S(1)} %get-tuple-element.20.refs_0_), channel_id=1, source_target_pairs={{0,2},{1,3},{2,0},{3,1},{4,6},{5,7},{6,4},{7,5},{8,10},{9,11},{10,... | collective-permute-start | bytes 393224 | tf_op jit(solution)/shard_map/ppermute | solution.py:457
  27.0 5.0 %collective-permute-start.7 = (f32[2,4,8,256]{3,2,1,0:T(8,128)S(1)}, f32[2,4,8,256]{3,2,1,0:T(8,128)S(1)}, u32[]{:S(2)}, u32[]{:S(2)}) collective-permute-start(f32[2,4,8,256]{3,2,1,0:T(8,128)S(1)} %edges.2.refs_0_), channel_id=1, source_target_pairs={{0,2},{1,3},{2,0},{3,1},{4,6},{5,7},{6,4},{7,5},{8,10},{9,11},{10,... | collective-permute-start | bytes 196616 | tf_op jit(solution)/shard_map/ppermute | solution.py:457
  29.6 3.6 %collective-permute-start.6 = (f32[2,4,8,256]{3,2,1,0:T(8,128)S(1)}, f32[2,4,8,256]{3,2,1,0:T(8,128)S(1)}, u32[]{:S(2)}, u32[]{:S(2)}) collective-permute-start(f32[2,4,8,256]{3,2,1,0:T(8,128)S(1)} %edges.3.home_ref), channel_id=1, source_target_pairs={{0,1},{1,0},{2,3},{3,2},{4,5},{5,4},{6,7},{7,6},{8,9},{9,8},{10,11... | collective-permute-start | bytes 196616 | tf_op jit(solution)/shard_map/ppermute | solution.py:368
  32.0 2.1 %collective-permute-start.8 = (f32[2,4,8,256]{3,2,1,0:T(8,128)S(1)}, f32[2,4,8,256]{3,2,1,0:T(8,128)S(1)}, u32[]{:S(2)}, u32[]{:S(2)}) collective-permute-start(f32[2,4,8,256]{3,2,1,0:T(8,128)S(1)} %collective-permute-done.7.across_ref), channel_id=1, source_target_pairs={{0,1},{1,0},{2,3},{3,2},{4,5},{5,4},{6,7},{7,6},{8,9},{9,8},{10,11... | collective-permute-start | bytes 196616 | tf_op jit(solution)/shard_map/ppermute | solution.py:368
where the time goes:
time: 35.3 us; the launch traced here: 34.8 us
  Pallas kernels  16.1 us (46%)
  starting transfers between devices  15.1 us (43%)
  waiting for transfers between devices  3.44 us (10%)
    ppermute x2, starting transfers between devices, swap_far(): lax.ppermute(x, axis, [(i, j) for k in range(1, size - 1, 2) for i, j in...  8.42 us
    pallas_call x1, Pallas kernels, local(): pl.pallas_call(functools.partial(middle_kernel, scale, slices, strips), o...  5.92 us
    ppermute x5, starting transfers between devices, swap_near(): lax.ppermute(x, axis, [(i, i ^ 1) for i in range(lax.axis_size(axis))])  5.1 us
    pallas_call x1, Pallas kernels, local(): pl.pallas_call(functools.partial(ends_kernel, scale, pieces, slices, stri...  3.67 us
    pallas_call x2, Pallas kernels, take_rows(): pl.pallas_call(functools.partial(rows_kernel, last_parity), out_shape=lat...  2.28 us
    pallas_call x2, Pallas kernels, edges_of(): pl.pallas_call(functools.partial(edge_kernel, pieces, first), out_shape=r...  2.21 us
    ppermute x5, waiting for transfers between devices, swap_near(): lax.ppermute(x, axis, [(i, i ^ 1) for i in range(lax.axis_size(axis))])  2.07 us
    ppermute x2, starting transfers between devices, swap_across(): return lax.ppermute(x, 'depth', [(i, i ^ 2) for i in range(pieces)])  1.57 us
  transfers between devices with their start and end apart: 9, of which 3 were waited for; matrix products, arithmetic and copies ran while one was open for 0% of the time, Pallas kernels for 41%

commit v1 on v0

--- a/solution.py
+++ b/solution.py
@@ -19,45 +19,56 @@
     return lax.broadcasted_iota(jnp.int32, shape, len(shape) - 2)
 
 
-def rows_kernel(last_parity, lat_ref, grade_hbm, amp_hbm, *refs):
-    out_ref, sems = refs[-2:]
+def take_kernel(lat_ref, depth_ref, grade_hbm, amp_hbm, pair_ref, cross_ref, near_ref, far_ref, sems, depth_sems):
     slices, rows = grade_hbm.shape[:2]
     span = slices // 4
-
-    def copies(first, places):
+    odd = lax.rem(depth_ref[0], 2)
+    fields = (grade_hbm, amp_hbm)
+
+    def copies(above_dst, below_dst):
         made = []
-        for f, src in enumerate((grade_hbm, amp_hbm)):
+        for f, src in enumerate(fields):
             for q in range(4):
-                here = src.at[pl.ds(span * q, span), pl.ds(first, 2), :]
-                made.append(pltpu.make_async_copy(here, out_ref.at[f, :, pl.ds(places[q], 2), :], sems.at[f, q]))
+                part = pl.ds(span * q, span)
+                above = above_dst.at[f, :, pl.ds((0, 6, 4, 2)[q], 2), :]
+                below = below_dst.at[f, :, pl.ds((6, 4, 2, 0)[q], 2), :]
+                made.append(pltpu.make_async_copy(src.at[part, pl.ds(rows - 2, 2), :], above, sems.at[f, q, 0]))
+                made.append(pltpu.make_async_copy(src.at[part, pl.ds(0, 2), :], below, sems.at[f, q, 1]))
+        for f, src in enumerate(fields):
+            for n, (dst, at) in enumerate(((near_ref, 1 - odd), (far_ref, odd))):
+                here = src.at[pl.ds(at * (slices - 2), 2)]
+                made.append(pltpu.make_async_copy(here, dst.at[f], depth_sems.at[f, n]))
         for copy in made:
             copy.start()
         for copy in made:
             copy.wait()
 
-    last = lax.rem(lat_ref[0], 2) == last_parity
-
-    @pl.when(last)
+    even = lax.rem(lat_ref[0], 2) == 0
+
+    @pl.when(even)
     def _():
-        copies(rows - 2, (0, 6, 4, 2))
-
-    @pl.when(jnp.logical_not(last))
+        copies(pair_ref, cross_ref)
+
+    @pl.when(jnp.logical_not(even))
     def _():
-        copies(0, (6, 4, 2, 0))
-
-
-def slices_kernel(depth_ref, grade_hbm, amp_hbm, after_ref, near_ref, far_ref, sems):
-    del after_ref
-    slices = grade_hbm.shape[0]
-    odd = lax.rem(depth_ref[0], 2)
-    made = []
-    for f, src in enumerate((grade_hbm, amp_hbm)):
-        for n, (dst, at) in enumerate(((near_ref, 1 - odd), (far_ref, odd))):
-            made.append(pltpu.make_async_copy(src.at[pl.ds(at * (slices - 2), 2)], dst.at[f], sems.at[f, n]))
-    for copy in made:
-        copy.start()
-    for copy in made:
-        copy.wait()
+        copies(cross_ref, pair_ref)
+
+
+def pass_on_kernel(*refs):
+    del refs
+
+
+def pass_on(x, *earlier):
+    spec = pl.BlockSpec(memory_space=pl.ANY)
+    return pl.pallas_call(
+        pass_on_kernel,
+        out_shape=jax.ShapeDtypeStruct(x.shape, x.dtype),
+        in_specs=[spec] * (1 + len(earlier)),
+        out_specs=spec,
+        input_output_aliases={0: 0},
+        compiler_params=pltpu.CompilerParams(vmem_limit_bytes=1 << 20),
+        name="pass_on",
+    )(x, *earlier)
 
 
 def round_weight(w):
@@ -175,21 +186,26 @@
                 for c in range(3):
                     mid_ref[rt, s, c] = zero
                 mid_ref[rt, s, 3] = zero + 1.0
-            for zb in range(2):
-                @pl.when(mask_ref[zb, rt, cb] != 0)
-                def _():
-                    for j in range(per_block):
-                        s = cb * per_block + j
-                        fields = [Field(ref, slices, strips, s) for ref in (grade_ref, amp_ref)]
-                        state = tuple(mid_ref[rt, s, c] for c in range(4))
+
+            def march(halves):
+                for j in range(per_block):
+                    s = cb * per_block + j
+                    fields = [Field(ref, slices, strips, s) for ref in (grade_ref, amp_ref)]
+                    state = (zero, zero, zero, zero + 1.0)
+                    for zb in halves:
                         for zi in range(2 - 2 * zb, MZ - 2 * zb):
                             z = zb * MZ + zi
                             along = [[field.load(z + k, rt) for k in (-2, -1, 1, 2)] for field in fields]
                             terms = cell_terms(fields, z, rt, along, False, bins, low_ref, high_ref)
                             keep(kept_ref, zi, s, rt, zb, terms)
                             state = step(state, terms)
-                        for c in range(4):
-                            mid_ref[rt, s, c] = state[c]
+                    for c in range(4):
+                        mid_ref[rt, s, c] = state[c]
+
+            front, back = mask_ref[0, rt, cb] != 0, mask_ref[1, rt, cb] != 0
+            pl.when(front & back)(functools.partial(march, (0, 1)))
+            pl.when(front & ~back)(functools.partial(march, (0,)))
+            pl.when(~front & back)(functools.partial(march, (1,)))
         return carry
 
     lax.fori_loop(0, strips // per_block, block, 0)
@@ -208,33 +224,26 @@
 
     def block(cb, carry):
         owner = lax.bitwise_xor(cb // piece_blocks, depth_ref[0])
-        for rt in range(2):
-            for zb in range(2):
-                if zb == 0:
-                    for j in range(per_block):
-                        for c in range(3):
-                            acc_ref[j, c] = zero
-                        acc_ref[j, 3] = zero + 1.0
-                else:
-                    for j in range(per_block):
-                        s = cb * per_block + j
-                        trans = acc_ref[j, 3]
-                        for c in range(3):
-                            acc_ref[j, c] = acc_ref[j, c] + trans * mid_ref[rt, s, c]
-                        acc_ref[j, 3] = trans * mid_ref[rt, s, 3]
-
-                @pl.when(mask_ref[zb, rt, cb] != 0)
-                def _():
-                    for j in range(per_block):
-                        s = cb * per_block + j
-                        fields = [Field(ref, slices, strips, s) for ref in (grade_ref, amp_ref)]
-                        halos = [[Field(ref, 4, strips, s) for ref in (near_ref, far_ref)]] * 2
-                        state = tuple(acc_ref[j, c] for c in range(4))
+        full = [[mask_ref[zb, rt, cb] for rt in range(2)] for zb in range(2)]
+
+        def march():
+            for rt in range(2):
+                for j in range(per_block):
+                    s = cb * per_block + j
+                    fields = [Field(ref, slices, strips, s) for ref in (grade_ref, amp_ref)]
+                    near, far = (Field(ref, 4, strips, s) for ref in (near_ref, far_ref))
+                    state = (zero, zero, zero, zero + 1.0)
+                    for zb in range(2):
+                        cover = jnp.broadcast_to(full[zb][rt], (SUB, LANES)).astype(jnp.float32)
+                        if zb == 1:
+                            red, green, blue, trans = state
+                            state = tuple(
+                                value + trans * mid_ref[rt, s, c] for c, value in enumerate((red, green, blue))
+                            ) + (trans * mid_ref[rt, s, 3],)
                         for zi in (0, 1) if zb == 0 else (MZ - 2, MZ - 1):
                             z = zb * MZ + zi
                             along = []
                             for f in range(2):
-                                near, far = halos[f]
 
                                 def at(z):
                                     if 0 <= z < slices:
@@ -246,17 +255,29 @@
                                 along.append([at(z + k) for k in (-2, -1, 1, 2)])
                             terms = cell_terms(fields, z, rt, along, True, bins, low_ref, high_ref)
                             keep(kept_ref, zi if zb == 0 else zi - 4, s, rt, zb, terms)
-                            state = step(state, terms)
-                        for c in range(4):
-                            acc_ref[j, c] = state[c]
-            for k, out in enumerate(outs):
-                @pl.when(lax.rem(owner, 2) == k)
-                def _():
+                            state = step(state, (*terms[:-1], terms[-1] * cover))
+                    for c in range(4):
+                        acc_ref[rt, j, c] = state[c]
+
+        some = (full[0][0] | full[0][1] | full[1][0] | full[1][1]) != 0
+        pl.when(some)(march)
+
+        @pl.when(jnp.logical_not(some))
+        def _():
+            for rt in range(2):
+                for j in range(per_block):
+                    for c in range(4):
+                        acc_ref[rt, j, c] = zero if c < 3 else zero + 1.0
+
+        for k, out in enumerate(outs):
+            @pl.when(lax.rem(owner, 2) == k)
+            def _():
+                for rt in range(2):
                     for c in range(4):
                         for j in range(per_block):
                             part = lax.rem(cb, piece_blocks) * MY + j * LANES
                             lanes = pl.ds(pl.multiple_of(part, LANES), LANES)
-                            out[owner // 2, c, rt * SUB:(rt + 1) * SUB, lanes] = acc_ref[j, c]
+                            out[owner // 2, c, rt * SUB:(rt + 1) * SUB, lanes] = acc_ref[rt, j, c]
         return carry
 
     lax.fori_loop(0, strips // per_block, block, 0)
@@ -397,29 +418,18 @@
     amplitude = pltpu.with_memory_space_constraint(amplitude, hbm_only)
     small = pltpu.CompilerParams(vmem_limit_bytes=4 << 20)
     after = pl.BlockSpec(memory_space=pl.ANY)
-
-    def take_rows(last_parity, *earlier):
-        return pl.pallas_call(
-            functools.partial(rows_kernel, last_parity),
-            out_shape=lat_halo,
-            in_specs=[smem, hbm, hbm] + [after] * len(earlier),
-            out_specs=vmem,
-            scratch_shapes=[pltpu.SemaphoreType.DMA((2, 4))],
-            compiler_params=small,
-            name="take_rows",
-        )(lat_rank, grade_field, amplitude, *earlier)
-
-    pair = take_rows(0)
-    near, far = pl.pallas_call(
-        slices_kernel,
-        out_shape=(depth_halo, depth_halo),
-        in_specs=[smem, hbm, hbm, after],
-        out_specs=[vmem, vmem],
-        scratch_shapes=[pltpu.SemaphoreType.DMA((2, 2))],
-        compiler_params=small,
-        name="take_slices",
-    )(depth_rank, grade_field, amplitude, pair)
-    cross = take_rows(1, far)
+    pair, cross, near, far = pl.pallas_call(
+        take_kernel,
+        out_shape=(lat_halo, lat_halo, depth_halo, depth_halo),
+        in_specs=[smem, smem, hbm, hbm],
+        out_specs=[vmem] * 4,
+        scratch_shapes=[pltpu.SemaphoreType.DMA((2, 4, 2)), pltpu.SemaphoreType.DMA((2, 2))],
+        compiler_params=pltpu.CompilerParams(vmem_limit_bytes=8 << 20),
+        name="take",
+    )(lat_rank, depth_rank, grade_field, amplitude)
+    far = pass_on(far, pair)
+    cross = pass_on(cross, far)
+    near = pass_on(near, cross)
     pair = swap_near(pair, "lat")
     cross = swap_far(cross, "lat")
     near = swap_near(near, "depth")
@@ -448,7 +458,7 @@
         out_shape=(half, half, jax.ShapeDtypeStruct((4, strips, TERMS, SUB, LANES), f32)),
         in_specs=[smem, smem] + [vmem] * 6,
         out_specs=[vmem] * 3,
-        scratch_shapes=[pltpu.VMEM((MY // LANES, 4, SUB, LANES), f32), table, table],
+        scratch_shapes=[pltpu.VMEM((2, MY // LANES, 4, SUB, LANES), f32), table, table],
         compiler_params=pltpu.CompilerParams(vmem_limit_bytes=8 << 20),
         name="ends",
     )(brick_mask, depth_rank, grade_strips, amp_strips, by_strips(near), by_strips(far), tf_table, mid)

time: 35.3 us -> 34.8 us (0.986)
  the two profiles are of different devices: /device:TPU:21 before, /device:TPU:0 now
where the time goes in v1:
time: 34.8 us; the launch traced here: 34.6 us
  Pallas kernels  15.1 us (43%)
  starting transfers between devices  11.5 us (33%)
  waiting for transfers between devices  7.92 us (23%)
    ppermute x5, starting transfers between devices, swap_near(): lax.ppermute(x, axis, [(i, i ^ 1) for i in range(lax.axis_size(axis))])  6.49 us
    ppermute x5, waiting for transfers between devices, swap_near(): lax.ppermute(x, axis, [(i, i ^ 1) for i in range(lax.axis_size(axis))])  6.31 us
    pallas_call x1, Pallas kernels, local(): pl.pallas_call(functools.partial(middle_kernel, scale, slices, strips), o...  5.88 us
    pallas_call x1, Pallas kernels, local(): pl.pallas_call(functools.partial(ends_kernel, scale, pieces, slices, stri...  4.53 us
    ppermute x2, starting transfers between devices, swap_across(): return lax.ppermute(x, 'depth', [(i, i ^ 2) for i in range(pieces)])  3.32 us
    pallas_call x2, Pallas kernels, edges_of(): pl.pallas_call(functools.partial(edge_kernel, pieces, first), out_shape=r...  2.16 us
    pallas_call x1, Pallas kernels, local(): pl.pallas_call(take_kernel, out_shape=(lat_halo, lat_halo, depth_halo, de...  1.79 us
    ppermute x2, starting transfers between devices, swap_far(): lax.ppermute(x, axis, [(i, j) for k in range(1, size - 1, 2) for i, j in...  1.65 us
  transfers between devices with their start and end apart: 9, of which 4 were waited for; matrix products, arithmetic and copies ran while one was open for 0% of the time, Pallas kernels for 36%

profile of v1, /device:TPU:0, one launch (start us, length us, event | category | flops | bytes accessed | tf_op | source)
XLA Modules:
  0.0 34.6 jit_solution(135750295542229021)
XLA Ops:
  0.0 1.8 %take.1 = (f32[2,4,8,2048]{3,2,1,0:T(8,128)S(1)}, f32[2,4,8,2048]{3,2,1,0:T(8,128)S(1)}, f32[2,2,16,2048]{3,2,1,0:T(8,128)S(1)}, f32[2,2,16,2048]{3,2,1,0:T(8,128)S(1)}) custom-call(s32[1]{0:T(128)} %bitcast.7.lat_ref, s32[1]{0:T(128)} %bitcast.depth_ref, f32[16,16,2048]{2,1,0:T(8,128)} %grade_hbm.1, f32[16,16,2048]{2,1,0:T(8,128)} %amp_hbm.1), custom_call_target="tpu_custom_call" | custom-call | tf_op jit(solution)/shard_map/take/pallas_call | solution.py:421
  1.8 3.0 %collective-permute-start.4 = (f32[2,4,8,2048]{3,2,1,0:T(8,128)S(1)}, f32[2,4,8,2048]{3,2,1,0:T(8,128)S(1)}, u32[]{:S(2)}, u32[]{:S(2)}) collective-permute-start(f32[2,4,8,2048]{3,2,1,0:T(8,128)S(1)} %get-tuple-element.19.refs_1_), channel_id=1, source_target_pairs={{0,4},{4,0},{8,12},{12,8},{16,20},{20,16},{24,28},{28,24},{1,5},{5... | collective-permute-start | bytes 1572872 | tf_op jit(solution)/shard_map/ppermute | solution.py:389
  4.8 0.0 copy-start
  4.8 0.0 copy-start.1
  4.8 0.0 copy-start.2
  4.8 0.0 copy-start.3
  4.9 0.8 %collective-permute-start.1 = (f32[2,2,16,2048]{3,2,1,0:T(8,128)S(1)}, f32[2,2,16,2048]{3,2,1,0:T(8,128)S(1)}, u32[]{:S(2)}, u32[]{:S(2)}) collective-permute-start(f32[2,2,16,2048]{3,2,1,0:T(8,128)S(1)} %pass_on.3.refs_1_), channel_id=1, source_target_pairs={{1,2},{2,1},{5,6},{6,5},{9,10},{10,9},{13,14},{14,13},{17,18},{18,... | collective-permute-start | bytes 1572872 | tf_op jit(solution)/shard_map/ppermute | solution.py:394
  5.7 0.8 %collective-permute-start.5 = (f32[2,4,8,2048]{3,2,1,0:T(8,128)S(1)}, f32[2,4,8,2048]{3,2,1,0:T(8,128)S(1)}, u32[]{:S(2)}, u32[]{:S(2)}) collective-permute-start(f32[2,4,8,2048]{3,2,1,0:T(8,128)S(1)} %pass_on.4.refs_1_), channel_id=1, source_target_pairs={{4,8},{8,4},{12,16},{16,12},{20,24},{24,20},{5,9},{9,5},{13,17},{1... | collective-permute-start | bytes 1572872 | tf_op jit(solution)/shard_map/ppermute | solution.py:394
  6.5 2.9 %collective-permute-start = (f32[2,2,16,2048]{3,2,1,0:T(8,128)S(1)}, f32[2,2,16,2048]{3,2,1,0:T(8,128)S(1)}, u32[]{:S(2)}, u32[]{:S(2)}) collective-permute-start(f32[2,2,16,2048]{3,2,1,0:T(8,128)S(1)} %pass_on.5), channel_id=1, source_target_pairs={{0,1},{1,0},{2,3},{3,2},{4,5},{5,4},{6,7},{7,6},{8,9},{9,8},{10,11... | collective-permute-start | bytes 1572872 | tf_op jit(solution)/shard_map/ppermute | solution.py:389
  9.4 0.0 copy-done
  9.4 0.0 copy-done.1
  9.4 0.0 copy-done.2
  9.4 0.0 copy-done.3
  9.4 5.9 %middle.1 = (f32[2,16,4,8,128]{4,3,2,1,0:T(8,128)S(1)}, f32[8,16,9,8,128]{4,3,2,1,0:T(8,128)S(1)}) custom-call(s32[2,2,8]{2,1,0:T(2,128)S(1)} %copy-done.2, f32[4096,128]{1,0:T(8,128)S(1)} %bitcast.22, f32[4096,128]{1,0:T(8,128)S(1)} %bitcast.24, s32[4,128]{1,0:T(4,128)S(1)} %copy-done.3), custom_call_target="tpu_custom_call" | custom-call | flops 10000000000 | bytes 100000000 | tf_op jit(solution)/shard_map/middle/pallas_call | solution.py:443
  15.3 0.0 collective-permute-done
  15.3 0.0 collective-permute-done.1
  15.4 4.5 %ends.1 = (f32[2,4,16,512]{3,2,1,0:T(8,128)S(1)}, f32[2,4,16,512]{3,2,1,0:T(8,128)S(1)}, f32[4,16,9,8,128]{4,3,2,1,0:T(8,128)S(1)}) custom-call(s32[2,2,8]{2,1,0:T(2,128)S(1)} %copy-done.2, s32[1]{0:T(128)} %bitcast.depth_ref, f32[4096,128]{1,0:T(8,128)S(1)} %bitcast.23, f32[4096,128]{1,0:T(8,128)S(1)} %bitcast.25, f32[1024,128]{1,0:T(8,128)S(1)} %bitcast.27, ...), custom_call_target="tpu_custom_call" | custom-call | tf_op jit(solution)/shard_map/ends/pallas_call | solution.py:456
  19.9 0.5 %collective-permute-start.2 = (f32[2,4,16,512]{3,2,1,0:T(8,128)S(1)}, f32[2,4,16,512]{3,2,1,0:T(8,128)S(1)}, u32[]{:S(2)}, u32[]{:S(2)}) collective-permute-start(f32[2,4,16,512]{3,2,1,0:T(8,128)S(1)} %get-tuple-element.22), channel_id=1, source_target_pairs={{0,1},{1,0},{2,3},{3,2},{4,5},{5,4},{6,7},{7,6},{8,9},{9,8},{10,11... | collective-permute-start | bytes 786440 | tf_op jit(solution)/shard_map/ppermute | solution.py:389
  20.4 1.2 %collective-permute-done.2.got_ref = f32[2,4,16,512]{3,2,1,0:T(8,128)S(1)} collective-permute-done((f32[2,4,16,512]{3,2,1,0:T(8,128)S(1)}, f32[2,4,16,512]{3,2,1,0:T(8,128)S(1)}, u32[]{:S(2)}, u32[]{:S(2)}) %collective-permute-start.2) | collective-permute-done | bytes 262176 | tf_op jit(solution)/shard_map/ppermute | solution.py:389
  21.6 1.8 %collective-permute-start.3 = (f32[4,16,512]{2,1,0:T(8,128)S(1)}, f32[4,16,512]{2,1,0:T(8,128)S(1)}, u32[]{:S(2)}, u32[]{:S(2)}) collective-permute-start(f32[4,16,512]{2,1,0:T(8,128)S(1)} %get-tuple-element.24.refs_0_), channel_id=1, source_target_pairs={{0,2},{1,3},{2,0},{3,1},{4,6},{5,7},{6,4},{7,5},{8,10},{9,11},{10,... | collective-permute-start | bytes 393224 | tf_op jit(solution)/shard_map/ppermute | solution.py:467
  23.4 0.0 collective-permute-done.5.cross_ref
  23.4 3.9 %collective-permute-done.4.pair_ref = f32[2,4,8,2048]{3,2,1,0:T(8,128)S(1)} collective-permute-done((f32[2,4,8,2048]{3,2,1,0:T(8,128)S(1)}, f32[2,4,8,2048]{3,2,1,0:T(8,128)S(1)}, u32[]{:S(2)}, u32[]{:S(2)}) %collective-permute-start.4) | collective-permute-done | bytes 524320 | tf_op jit(solution)/shard_map/ppermute | solution.py:389
  27.3 1.1 %edges.2.refs_0_ = f32[2,4,8,256]{3,2,1,0:T(8,128)S(1)} custom-call(s32[2,2,8]{2,1,0:T(2,128)S(1)} %copy-done.2, s32[1]{0:T(128)} %bitcast.depth_ref, s32[1]{0:T(128)} %bitcast.7.lat_ref, f32[8,16,9,8,128]{4,3,2,1,0:T(8,128)S(1)} %get-tuple-element.25.kept_ref, f32[4,16,9,8,128]{4,3,2,1,0:T(8,128)S(1)} %get-tuple-element.26.ends_ref, ...), custom_call_target="tpu_custom_call" | custom-call | tf_op jit(solution)/shard_map/edges/pallas_call | solution.py:481
  28.3 1.6 %collective-permute-start.7 = (f32[2,4,8,256]{3,2,1,0:T(8,128)S(1)}, f32[2,4,8,256]{3,2,1,0:T(8,128)S(1)}, u32[]{:S(2)}, u32[]{:S(2)}) collective-permute-start(f32[2,4,8,256]{3,2,1,0:T(8,128)S(1)} %edges.2.refs_0_), channel_id=1, source_target_pairs={{0,2},{1,3},{2,0},{3,1},{4,6},{5,7},{6,4},{7,5},{8,10},{9,11},{10,... | collective-permute-start | bytes 196616 | tf_op jit(solution)/shard_map/ppermute | solution.py:467
  29.9 1.1 %edges.3.home_ref = f32[2,4,8,256]{3,2,1,0:T(8,128)S(1)} custom-call(s32[2,2,8]{2,1,0:T(2,128)S(1)} %copy-done.2, s32[1]{0:T(128)} %bitcast.depth_ref, s32[1]{0:T(128)} %bitcast.7.lat_ref, f32[8,16,9,8,128]{4,3,2,1,0:T(8,128)S(1)} %get-tuple-element.25.kept_ref, f32[4,16,9,8,128]{4,3,2,1,0:T(8,128)S(1)} %get-tuple-element.26.ends_ref, ...), custom_call_target="tpu_custom_call" | custom-call | tf_op jit(solution)/shard_map/edges/pallas_call | solution.py:481
  31.0 0.1 collective-permute-start.6
  31.1 1.6 %collective-permute-done.7.across_ref = f32[2,4,8,256]{3,2,1,0:T(8,128)S(1)} collective-permute-done((f32[2,4,8,256]{3,2,1,0:T(8,128)S(1)}, f32[2,4,8,256]{3,2,1,0:T(8,128)S(1)}, u32[]{:S(2)}, u32[]{:S(2)}) %collective-permute-start.7) | collective-permute-done | bytes 65568 | tf_op jit(solution)/shard_map/ppermute | solution.py:467
  32.7 0.0 collective-permute-start.8
  32.7 0.0 collective-permute-done.6.beside_ref
  32.7 0.0 collective-permute-done.3.got_ref
  32.7 1.2 %collective-permute-done.8.corner_ref = f32[2,4,8,256]{3,2,1,0:T(8,128)S(1)} collective-permute-done((f32[2,4,8,256]{3,2,1,0:T(8,128)S(1)}, f32[2,4,8,256]{3,2,1,0:T(8,128)S(1)}, u32[]{:S(2)}, u32[]{:S(2)}) %collective-permute-start.8) | collective-permute-done | bytes 65568 | tf_op jit(solution)/shard_map/ppermute | solution.py:389
  33.9 0.7 %finish.1 = f32[4,16,512]{2,1,0:T(8,128)} custom-call(s32[1]{0:T(128)} %bitcast.depth_ref, f32[4,16,512]{2,1,0:T(8,128)S(1)} %get-tuple-element.23.own_ref, f32[4,16,512]{2,1,0:T(8,128)S(1)} %collective-permute-done.3.got_ref, f32[2,4,8,256]{3,2,1,0:T(8,128)S(1)} %edges.3.home_ref, f32[2,4,8,256]{3,2,1,0:T(8,128)S(1)} %collective-permute-done.6.beside_ref, ...), custom_call_target="tpu_custom_call" | custom-call | tf_op jit(solution)/shard_map/finish/pallas_call | solution.py:494
  (4 shorter events, 0.0 us)
Async XLA Ops:
  1.8 25.5 %collective-permute-start.4 = (f32[2,4,8,2048]{3,2,1,0:T(8,128)S(1)}, f32[2,4,8,2048]{3,2,1,0:T(8,128)S(1)}, u32[]{:S(2)}, u32[]{:S(2)}) collective-permute-start(f32[2,4,8,2048]{3,2,1,0:T(8,128)S(1)} %get-tuple-element.19.refs_1_), channel_id=1, source_target_pairs={{0,4},{4,0},{8,12},{12,8},{16,20},{20,16},{24,28},{28,24},{1,5},{5... | collective-permute-start | bytes 1572872 | tf_op jit(solution)/shard_map/ppermute | solution.py:389
  4.8 4.6 %copy-start = (f32[16,16,2048]{2,1,0:T(8,128)S(1)}, f32[16,16,2048]{2,1,0:T(8,128)}, u32[]{:S(2)}) copy-start(f32[16,16,2048]{2,1,0:T(8,128)} %grade_hbm.1) | copy-start | bytes 6291460
  4.8 4.6 %copy-start.1 = (f32[16,16,2048]{2,1,0:T(8,128)S(1)}, f32[16,16,2048]{2,1,0:T(8,128)}, u32[]{:S(2)}) copy-start(f32[16,16,2048]{2,1,0:T(8,128)} %amp_hbm.1) | copy-start | bytes 6291460
  4.8 4.6 %copy-start.2 = (s32[2,2,8]{2,1,0:T(2,128)S(1)}, s32[2,2,8]{2,1,0:T(2,128)}, u32[]{:S(2)}) copy-start(s32[2,2,8]{2,1,0:T(2,128)} %mask_ref.7) | copy-start | bytes 388
  4.8 4.6 %copy-start.3 = (s32[4,128]{1,0:T(4,128)S(1)}, s32[4,128]{1,0:T(4,128)}, u32[]{:S(2)}) copy-start(s32[4,128]{1,0:T(4,128)} %table_ref.3) | copy-start | bytes 6148
  4.9 10.5 %collective-permute-start.1 = (f32[2,2,16,2048]{3,2,1,0:T(8,128)S(1)}, f32[2,2,16,2048]{3,2,1,0:T(8,128)S(1)}, u32[]{:S(2)}, u32[]{:S(2)}) collective-permute-start(f32[2,2,16,2048]{3,2,1,0:T(8,128)S(1)} %pass_on.3.refs_1_), channel_id=1, source_target_pairs={{1,2},{2,1},{5,6},{6,5},{9,10},{10,9},{13,14},{14,13},{17,18},{18,... | collective-permute-start | bytes 1572872 | tf_op jit(solution)/shard_map/ppermute | solution.py:394
  5.7 17.7 %collective-permute-start.5 = (f32[2,4,8,2048]{3,2,1,0:T(8,128)S(1)}, f32[2,4,8,2048]{3,2,1,0:T(8,128)S(1)}, u32[]{:S(2)}, u32[]{:S(2)}) collective-permute-start(f32[2,4,8,2048]{3,2,1,0:T(8,128)S(1)} %pass_on.4.refs_1_), channel_id=1, source_target_pairs={{4,8},{8,4},{12,16},{16,12},{20,24},{24,20},{5,9},{9,5},{13,17},{1... | collective-permute-start | bytes 1572872 | tf_op jit(solution)/shard_map/ppermute | solution.py:394
  6.5 8.8 %collective-permute-start = (f32[2,2,16,2048]{3,2,1,0:T(8,128)S(1)}, f32[2,2,16,2048]{3,2,1,0:T(8,128)S(1)}, u32[]{:S(2)}, u32[]{:S(2)}) collective-permute-start(f32[2,2,16,2048]{3,2,1,0:T(8,128)S(1)} %pass_on.5), channel_id=1, source_target_pairs={{0,1},{1,0},{2,3},{3,2},{4,5},{5,4},{6,7},{7,6},{8,9},{9,8},{10,11... | collective-permute-start | bytes 1572872 | tf_op jit(solution)/shard_map/ppermute | solution.py:389
  19.9 1.7 %collective-permute-start.2 = (f32[2,4,16,512]{3,2,1,0:T(8,128)S(1)}, f32[2,4,16,512]{3,2,1,0:T(8,128)S(1)}, u32[]{:S(2)}, u32[]{:S(2)}) collective-permute-start(f32[2,4,16,512]{3,2,1,0:T(8,128)S(1)} %get-tuple-element.22), channel_id=1, source_target_pairs={{0,1},{1,0},{2,3},{3,2},{4,5},{5,4},{6,7},{7,6},{8,9},{9,8},{10,11... | collective-permute-start | bytes 786440 | tf_op jit(solution)/shard_map/ppermute | solution.py:389
  21.6 11.1 %collective-permute-start.3 = (f32[4,16,512]{2,1,0:T(8,128)S(1)}, f32[4,16,512]{2,1,0:T(8,128)S(1)}, u32[]{:S(2)}, u32[]{:S(2)}) collective-permute-start(f32[4,16,512]{2,1,0:T(8,128)S(1)} %get-tuple-element.24.refs_0_), channel_id=1, source_target_pairs={{0,2},{1,3},{2,0},{3,1},{4,6},{5,7},{6,4},{7,5},{8,10},{9,11},{10,... | collective-permute-start | bytes 393224 | tf_op jit(solution)/shard_map/ppermute | solution.py:467
  28.3 4.3 %collective-permute-start.7 = (f32[2,4,8,256]{3,2,1,0:T(8,128)S(1)}, f32[2,4,8,256]{3,2,1,0:T(8,128)S(1)}, u32[]{:S(2)}, u32[]{:S(2)}) collective-permute-start(f32[2,4,8,256]{3,2,1,0:T(8,128)S(1)} %edges.2.refs_0_), channel_id=1, source_target_pairs={{0,2},{1,3},{2,0},{3,1},{4,6},{5,7},{6,4},{7,5},{8,10},{9,11},{10,... | collective-permute-start | bytes 196616 | tf_op jit(solution)/shard_map/ppermute | solution.py:467
  31.0 1.7 %collective-permute-start.6 = (f32[2,4,8,256]{3,2,1,0:T(8,128)S(1)}, f32[2,4,8,256]{3,2,1,0:T(8,128)S(1)}, u32[]{:S(2)}, u32[]{:S(2)}) collective-permute-start(f32[2,4,8,256]{3,2,1,0:T(8,128)S(1)} %edges.3.home_ref), channel_id=1, source_target_pairs={{0,1},{1,0},{2,3},{3,2},{4,5},{5,4},{6,7},{7,6},{8,9},{9,8},{10,11... | collective-permute-start | bytes 196616 | tf_op jit(solution)/shard_map/ppermute | solution.py:389
  32.7 1.3 %collective-permute-start.8 = (f32[2,4,8,256]{3,2,1,0:T(8,128)S(1)}, f32[2,4,8,256]{3,2,1,0:T(8,128)S(1)}, u32[]{:S(2)}, u32[]{:S(2)}) collective-permute-start(f32[2,4,8,256]{3,2,1,0:T(8,128)S(1)} %collective-permute-done.7.across_ref), channel_id=1, source_target_pairs={{0,1},{1,0},{2,3},{3,2},{4,5},{5,4},{6,7},{7,6},{8,9},{9,8},{10,11... | collective-permute-start | bytes 196616 | tf_op jit(solution)/shard_map/ppermute | solution.py:389

commit v2 on v1

--- a/solution.py
+++ b/solution.py
@@ -19,39 +19,50 @@
     return lax.broadcasted_iota(jnp.int32, shape, len(shape) - 2)
 
 
-def take_kernel(lat_ref, depth_ref, grade_hbm, amp_hbm, pair_ref, cross_ref, near_ref, far_ref, sems, depth_sems):
-    slices, rows = grade_hbm.shape[:2]
+PLACES = ((6, 4, 2, 0), (0, 6, 4, 2))
+
+
+def row_copies(fields, out_ref, sems, last):
+    slices, rows = fields[0].shape[:2]
     span = slices // 4
+    made = []
+    for f, src in enumerate(fields):
+        for q in range(4):
+            here = src.at[pl.ds(span * q, span), pl.ds(rows - 2 if last else 0, 2), :]
+            made.append(pltpu.make_async_copy(here, out_ref.at[f, :, pl.ds(PLACES[last][q], 2), :], sems.at[f, q]))
+    return made
+
+
+def start_and_wait(copies):
+    for copy in copies:
+        copy.start()
+    for copy in copies:
+        copy.wait()
+
+
+def pair_kernel(lat_ref, grade_hbm, amp_hbm, pair_ref, sems):
+    odd = lax.rem(lat_ref[0], 2)
+    for last in (0, 1):
+        @pl.when(odd == 1 - last)
+        def _():
+            start_and_wait(row_copies((grade_hbm, amp_hbm), pair_ref, sems, last))
+
+
+def rest_kernel(lat_ref, depth_ref, grade_hbm, amp_hbm, after_ref, cross_ref, near_ref, far_ref, sems, depth_sems):
+    del after_ref
+    slices = grade_hbm.shape[0]
+    fields = (grade_hbm, amp_hbm)
     odd = lax.rem(depth_ref[0], 2)
-    fields = (grade_hbm, amp_hbm)
-
-    def copies(above_dst, below_dst):
-        made = []
-        for f, src in enumerate(fields):
-            for q in range(4):
-                part = pl.ds(span * q, span)
-                above = above_dst.at[f, :, pl.ds((0, 6, 4, 2)[q], 2), :]
-                below = below_dst.at[f, :, pl.ds((6, 4, 2, 0)[q], 2), :]
-                made.append(pltpu.make_async_copy(src.at[part, pl.ds(rows - 2, 2), :], above, sems.at[f, q, 0]))
-                made.append(pltpu.make_async_copy(src.at[part, pl.ds(0, 2), :], below, sems.at[f, q, 1]))
-        for f, src in enumerate(fields):
-            for n, (dst, at) in enumerate(((near_ref, 1 - odd), (far_ref, odd))):
-                here = src.at[pl.ds(at * (slices - 2), 2)]
-                made.append(pltpu.make_async_copy(here, dst.at[f], depth_sems.at[f, n]))
-        for copy in made:
-            copy.start()
-        for copy in made:
-            copy.wait()
-
-    even = lax.rem(lat_ref[0], 2) == 0
-
-    @pl.when(even)
-    def _():
-        copies(pair_ref, cross_ref)
-
-    @pl.when(jnp.logical_not(even))
-    def _():
-        copies(cross_ref, pair_ref)
+    parallel = []
+    for f, src in enumerate(fields):
+        for n, (dst, at) in enumerate(((near_ref, 1 - odd), (far_ref, odd))):
+            here = src.at[pl.ds(at * (slices - 2), 2)]
+            parallel.append(pltpu.make_async_copy(here, dst.at[f], depth_sems.at[f, n]))
+    odd_lat = lax.rem(lat_ref[0], 2)
+    for last in (0, 1):
+        @pl.when(odd_lat == last)
+        def _():
+            start_and_wait(row_copies(fields, cross_ref, sems, last) + parallel)
 
 
 def pass_on_kernel(*refs):
@@ -173,6 +184,15 @@
         kept_ref[zi, s, n, at:at + 2, :] = term[rows, :]
 
 
+BLANK = (0.0, 0.0, 36.0, 144.0, 0.0, 0.0, 0.0, 0.0, 0.0)
+
+
+def blank(kept_ref, zi, s, rt, zb):
+    at = KEPT_AT[rt][zb]
+    for n, value in enumerate(BLANK):
+        kept_ref[zi, s, n, at:at + 2, :] = jnp.full((2, LANES), value, jnp.float32)
+
+
 def middle_kernel(scale, slices, strips, mask_ref, grade_ref, amp_ref, table_ref, mid_ref, kept_ref, low_ref, high_ref):
     bins = table_ref.shape[1]
     fill_tables(scale, table_ref, low_ref, high_ref)
@@ -181,12 +201,6 @@
 
     def block(cb, carry):
         for rt in range(2):
-            for j in range(per_block):
-                s = cb * per_block + j
-                for c in range(3):
-                    mid_ref[rt, s, c] = zero
-                mid_ref[rt, s, 3] = zero + 1.0
-
             def march(halves):
                 for j in range(per_block):
                     s = cb * per_block + j
@@ -199,6 +213,9 @@
                             terms = cell_terms(fields, z, rt, along, False, bins, low_ref, high_ref)
                             keep(kept_ref, zi, s, rt, zb, terms)
                             state = step(state, terms)
+                    for zb in {0, 1} - set(halves):
+                        for zi in range(2 - 2 * zb, MZ - 2 * zb):
+                            blank(kept_ref, zi, s, rt, zb)
                     for c in range(4):
                         mid_ref[rt, s, c] = state[c]
 
@@ -206,13 +223,14 @@
             pl.when(front & back)(functools.partial(march, (0, 1)))
             pl.when(front & ~back)(functools.partial(march, (0,)))
             pl.when(~front & back)(functools.partial(march, (1,)))
+            pl.when(~front & ~back)(functools.partial(march, ()))
         return carry
 
     lax.fori_loop(0, strips // per_block, block, 0)
 
 
 def ends_kernel(scale, pieces, slices, strips, mask_ref, depth_ref, grade_ref, amp_ref, near_ref, far_ref, table_ref,
-                mid_ref, *rest):
+                mid_ref, middle_kept_ref, *rest):
     outs, (kept_ref, acc_ref, low_ref, high_ref) = rest[:2], rest[2:]
     bins = table_ref.shape[1]
     fill_tables(scale, table_ref, low_ref, high_ref)
@@ -227,6 +245,11 @@
         full = [[mask_ref[zb, rt, cb] for rt in range(2)] for zb in range(2)]
 
         def march():
+            for j in range(per_block):
+                s = cb * per_block + j
+                for n in range(TERMS):
+                    for k, zi in enumerate((0, 1, MZ - 2, MZ - 1)):
+                        kept_ref[k, s, n] = middle_kept_ref[zi, s, n]
             for rt in range(2):
                 for j in range(per_block):
                     s = cb * per_block + j
@@ -254,8 +277,9 @@
 
                                 along.append([at(z + k) for k in (-2, -1, 1, 2)])
                             terms = cell_terms(fields, z, rt, along, True, bins, low_ref, high_ref)
+                            terms = (*terms[:-1], terms[-1] * cover)
                             keep(kept_ref, zi if zb == 0 else zi - 4, s, rt, zb, terms)
-                            state = step(state, (*terms[:-1], terms[-1] * cover))
+                            state = step(state, terms)
                     for c in range(4):
                         acc_ref[rt, j, c] = state[c]
 
@@ -264,6 +288,10 @@
 
         @pl.when(jnp.logical_not(some))
         def _():
+            for j in range(per_block):
+                for n, value in enumerate(BLANK):
+                    for k in range(4):
+                        kept_ref[k, cb * per_block + j, n] = jnp.full((SUB, LANES), value, jnp.float32)
             for rt in range(2):
                 for j in range(per_block):
                     for c in range(4):
@@ -283,7 +311,7 @@
     lax.fori_loop(0, strips // per_block, block, 0)
 
 
-def edge_kernel(pieces, first, mask_ref, depth_ref, lat_ref, kept_ref, ends_ref, pair_ref, cross_ref, *refs):
+def edge_kernel(pieces, first, depth_ref, lat_ref, kept_ref, ends_ref, pair_ref, cross_ref, *refs):
     out_ref = refs[-1]
     half = kept_ref.shape[0]
     strips = kept_ref.shape[1]
@@ -297,42 +325,28 @@
     above = lax.rem(sub // 2, 2) == 0
     even_row = lax.rem(sub, 2) == 0
 
-    def outside(raw, above):
+    own_factor = jnp.where(above, 1.0, -1.0)
+    mate_factor = jnp.where(above == even_row, -8.0 * own_factor, 0.0)
+
+    def outside(raw):
         mate = jnp.where(even_row, pltpu.roll(raw, SUB - 1, 0), pltpu.roll(raw, 1, 0))
-        mate = jnp.where(above == even_row, 8.0 * mate, 0.0)
-        return jnp.where(above, raw - mate, mate - raw)
+        return own_factor * raw + mate_factor * mate
 
     def halo(f, zi, lanes):
         pair, cross = pair_ref[f, zi % 4, :, lanes], cross_ref[f, zi % 4, :, lanes]
         if zi < 4:
-            return outside(jnp.where(from_pair, pair, cross), above)
-        return outside(pltpu.roll(jnp.where(from_pair, cross, pair), 2, 0), above)
+            return outside(jnp.where(from_pair, pair, cross))
+        return outside(pltpu.roll(jnp.where(from_pair, cross, pair), 2, 0))
 
     def strip(s):
         lanes = pl.ds(pl.multiple_of(s * LANES, LANES), LANES)
-        cb = s // (MY // LANES)
-        full = [[jnp.broadcast_to(mask_ref[zb, rt, cb], (SUB, LANES)) for rt in range(2)] for zb in range(2)]
-        live = jnp.where(
-            sub < 4, jnp.where(sub < 2, full[0][0], full[1][1]), jnp.where(sub < 6, full[1][0], full[0][1])
-        ) != 0
         zero = jnp.zeros((SUB, LANES), jnp.float32)
-        total = [zero, zero, zero]
-        trans = zero + 1.0
+        state = (zero, zero, zero, zero + 1.0)
         for zi in range(half):
-            terms = [kept_ref[zi, s, n] for n in range(TERMS)]
-            if zi < 2:
-                terms = [jnp.where(is_first, ends_ref[zi, s, n], term) for n, term in enumerate(terms)]
-            if zi >= half - 2:
-                terms = [jnp.where(is_first, term, ends_ref[zi - half + 4, s, n]) for n, term in enumerate(terms)]
-            g_x, a_x, g_yz, a_yz, steep, red, green, blue, alpha = terms
-            g_x = g_x + halo(0, zi, lanes)
-            a_x = a_x + halo(1, zi, lanes)
-            edge = 1.0 - 12.0 * lax.rsqrt(a_x * a_x + a_yz)
-            shade = 0.3 + steep * lax.rsqrt(g_x * g_x + g_yz)
-            weight = jnp.where(live, trans * (alpha * edge), 0.0)
-            trans = trans - weight
-            weight = weight * shade
-            total = [t + jnp.where(live, weight * c, 0.0) for t, c in zip(total, (red, green, blue))]
+            held, at = (kept_ref, zi) if 2 <= zi < half - 2 else (ends_ref, zi % (half - 4))
+            g_x, a_x, *others = (held[at, s, n] for n in range(TERMS))
+            state = step(state, (g_x + halo(0, zi, lanes), a_x + halo(1, zi, lanes), *others))
+        *total, trans = state
         out = [t + trans * pltpu.roll(t, 4, 0) for t in total]
         return out + [trans * pltpu.roll(trans, 4, 0)]
 
@@ -418,18 +432,26 @@
     amplitude = pltpu.with_memory_space_constraint(amplitude, hbm_only)
     small = pltpu.CompilerParams(vmem_limit_bytes=4 << 20)
     after = pl.BlockSpec(memory_space=pl.ANY)
-    pair, cross, near, far = pl.pallas_call(
-        take_kernel,
-        out_shape=(lat_halo, lat_halo, depth_halo, depth_halo),
-        in_specs=[smem, smem, hbm, hbm],
-        out_specs=[vmem] * 4,
-        scratch_shapes=[pltpu.SemaphoreType.DMA((2, 4, 2)), pltpu.SemaphoreType.DMA((2, 2))],
-        compiler_params=pltpu.CompilerParams(vmem_limit_bytes=8 << 20),
-        name="take",
-    )(lat_rank, depth_rank, grade_field, amplitude)
-    far = pass_on(far, pair)
-    cross = pass_on(cross, far)
-    near = pass_on(near, cross)
+    pair = pl.pallas_call(
+        pair_kernel,
+        out_shape=lat_halo,
+        in_specs=[smem, hbm, hbm],
+        out_specs=vmem,
+        scratch_shapes=[pltpu.SemaphoreType.DMA((2, 4))],
+        compiler_params=small,
+        name="take_pair",
+    )(lat_rank, grade_field, amplitude)
+    cross, near, far = pl.pallas_call(
+        rest_kernel,
+        out_shape=(lat_halo, depth_halo, depth_halo),
+        in_specs=[smem, smem, hbm, hbm, after],
+        out_specs=[vmem] * 3,
+        scratch_shapes=[pltpu.SemaphoreType.DMA((2, 4)), pltpu.SemaphoreType.DMA((2, 2))],
+        compiler_params=small,
+        name="take_rest",
+    )(lat_rank, depth_rank, grade_field, amplitude, pair)
+    far = pass_on(far, cross)
+    near = pass_on(near, far)
     pair = swap_near(pair, "lat")
     cross = swap_far(cross, "lat")
     near = swap_near(near, "depth")
@@ -456,12 +478,12 @@
     stay, go, kept_ends = pl.pallas_call(
         functools.partial(ends_kernel, scale, pieces, slices, strips),
         out_shape=(half, half, jax.ShapeDtypeStruct((4, strips, TERMS, SUB, LANES), f32)),
-        in_specs=[smem, smem] + [vmem] * 6,
+        in_specs=[smem, smem] + [vmem] * 7,
         out_specs=[vmem] * 3,
         scratch_shapes=[pltpu.VMEM((2, MY // LANES, 4, SUB, LANES), f32), table, table],
         compiler_params=pltpu.CompilerParams(vmem_limit_bytes=8 << 20),
         name="ends",
-    )(brick_mask, depth_rank, grade_strips, amp_strips, by_strips(near), by_strips(far), tf_table, mid)
+    )(brick_mask, depth_rank, grade_strips, amp_strips, by_strips(near), by_strips(far), tf_table, mid, kept)
 
     def swap_across(x):
         return lax.ppermute(x, "depth", [(i, i ^ 2) for i in range(pieces)])
@@ -481,11 +503,11 @@
         return pl.pallas_call(
             functools.partial(edge_kernel, pieces, first),
             out_shape=rims,
-            in_specs=[smem, smem, smem, vmem, vmem, vmem, vmem] + [after] * len(earlier),
+            in_specs=[smem, smem, vmem, vmem, vmem, vmem] + [after] * len(earlier),
             out_specs=vmem,
             compiler_params=small,
             name="edges",
-        )(brick_mask, depth_rank, lat_rank, kept, kept_ends, pair, cross, *earlier)
+        )(depth_rank, lat_rank, kept, kept_ends, pair, cross, *earlier)
 
     away = edges_of(2, away_inner)
     home = edges_of(0, away)

time: 34.8 us -> 34.4 us (0.989)
  the two profiles are of different devices: /device:TPU:0 before, /device:TPU:21 now
where the time goes in v2:
time: 34.4 us; the launch traced here: 33.8 us
  Pallas kernels  14.8 us (43%)
  starting transfers between devices  13.6 us (40%)
  waiting for transfers between devices  5.23 us (15%)
    ppermute x2, starting transfers between devices, swap_far(): lax.ppermute(x, axis, [(i, j) for k in range(1, size - 1, 2) for i, j in...  8.53 us
    pallas_call x1, Pallas kernels, local(): pl.pallas_call(functools.partial(middle_kernel, scale, slices, strips), o...  6.39 us
    pallas_call x1, Pallas kernels, local(): pl.pallas_call(functools.partial(ends_kernel, scale, pieces, slices, stri...  4.15 us
    ppermute x5, starting transfers between devices, swap_near(): lax.ppermute(x, axis, [(i, i ^ 1) for i in range(lax.axis_size(axis))])  3.21 us
    ppermute x5, waiting for transfers between devices, swap_near(): lax.ppermute(x, axis, [(i, i ^ 1) for i in range(lax.axis_size(axis))])  2.43 us
    ppermute x2, waiting for transfers between devices, swap_across(): return lax.ppermute(x, 'depth', [(i, i ^ 2) for i in range(pieces)])  2.19 us
    ppermute x2, starting transfers between devices, swap_across(): return lax.ppermute(x, 'depth', [(i, i ^ 2) for i in range(pieces)])  1.82 us
    pallas_call x1, Pallas kernels, local(): pl.pallas_call(rest_kernel, out_shape=(lat_halo, depth_halo, depth_halo),...  1.69 us
  transfers between devices with their start and end apart: 9, of which 4 were waited for; matrix products, arithmetic and copies ran while one was open for 0% of the time, Pallas kernels for 38%

profile of v2, /device:TPU:21, one launch (start us, length us, event | category | flops | bytes accessed | tf_op | source)
XLA Modules:
  0.0 33.8 jit_solution(8472603562571791907)
XLA Ops:
  0.0 1.1 %take_pair.1.after_ref = f32[2,4,8,2048]{3,2,1,0:T(8,128)S(1)} custom-call(s32[1]{0:T(128)} %bitcast.7.lat_ref, f32[16,16,2048]{2,1,0:T(8,128)} %grade_hbm.3, f32[16,16,2048]{2,1,0:T(8,128)} %amp_hbm.3), custom_call_target="tpu_custom_call" | custom-call | tf_op jit(solution)/shard_map/take_pair/pallas_call | solution.py:435
  1.1 0.3 collective-permute-start.4
  1.4 0.0 copy-start.1
  1.4 1.7 %take_rest.1 = (f32[2,4,8,2048]{3,2,1,0:T(8,128)S(1)}, f32[2,2,16,2048]{3,2,1,0:T(8,128)S(1)}, f32[2,2,16,2048]{3,2,1,0:T(8,128)S(1)}) custom-call(s32[1]{0:T(128)} %bitcast.7.lat_ref, s32[1]{0:T(128)} %bitcast.depth_ref, f32[16,16,2048]{2,1,0:T(8,128)} %grade_hbm.3, f32[16,16,2048]{2,1,0:T(8,128)} %amp_hbm.3, f32[2,4,8,2048]{3,2,1,0:T(8,128)S(1)} %take_pair.1.after_ref), custom_call_target="tpu_custom_call" | custom-call | tf_op jit(solution)/shard_map/take_rest/pallas_call | solution.py:444
  3.1 0.0 copy-start
  3.1 0.0 copy-start.2
  3.2 0.0 copy-start.3
  3.2 4.3 %collective-permute-start.5 = (f32[2,4,8,2048]{3,2,1,0:T(8,128)S(1)}, f32[2,4,8,2048]{3,2,1,0:T(8,128)S(1)}, u32[]{:S(2)}, u32[]{:S(2)}) collective-permute-start(f32[2,4,8,2048]{3,2,1,0:T(8,128)S(1)} %get-tuple-element.17.refs_1_), channel_id=1, source_target_pairs={{4,8},{8,4},{12,16},{16,12},{20,24},{24,20},{5,9},{9,5},{13,17},{1... | collective-permute-start | bytes 1572872 | tf_op jit(solution)/shard_map/ppermute | solution.py:408
  7.5 4.2 %collective-permute-start.1 = (f32[2,2,16,2048]{3,2,1,0:T(8,128)S(1)}, f32[2,2,16,2048]{3,2,1,0:T(8,128)S(1)}, u32[]{:S(2)}, u32[]{:S(2)}) collective-permute-start(f32[2,2,16,2048]{3,2,1,0:T(8,128)S(1)} %pass_on.2.refs_1_), channel_id=1, source_target_pairs={{1,2},{2,1},{5,6},{6,5},{9,10},{10,9},{13,14},{14,13},{17,18},{18,... | collective-permute-start | bytes 1572872 | tf_op jit(solution)/shard_map/ppermute | solution.py:408
  11.7 0.1 collective-permute-start
  11.8 0.0 copy-done.1
  11.8 0.0 copy-done
  11.8 0.0 copy-done.2
  11.8 0.0 copy-done.3
  11.9 6.4 %middle.1 = (f32[2,16,4,8,128]{4,3,2,1,0:T(8,128)S(1)}, f32[8,16,9,8,128]{4,3,2,1,0:T(8,128)S(1)}) custom-call(s32[2,2,8]{2,1,0:T(2,128)S(1)} %copy-done.2, f32[4096,128]{1,0:T(8,128)S(1)} %bitcast.22, f32[4096,128]{1,0:T(8,128)S(1)} %bitcast.24, s32[4,128]{1,0:T(4,128)S(1)} %copy-done.3), custom_call_target="tpu_custom_call" | custom-call | flops 10000000000 | bytes 100000000 | tf_op jit(solution)/shard_map/middle/pallas_call | solution.py:465
  18.3 0.0 collective-permute-done
  18.3 0.6 %collective-permute-done.1 = f32[2,2,16,2048]{3,2,1,0:T(8,128)S(1)} collective-permute-done((f32[2,2,16,2048]{3,2,1,0:T(8,128)S(1)}, f32[2,2,16,2048]{3,2,1,0:T(8,128)S(1)}, u32[]{:S(2)}, u32[]{:S(2)}) %collective-permute-start.1) | collective-permute-done | bytes 524320 | tf_op jit(solution)/shard_map/ppermute | solution.py:408
  18.9 4.2 %ends.1 = (f32[2,4,16,512]{3,2,1,0:T(8,128)S(1)}, f32[2,4,16,512]{3,2,1,0:T(8,128)S(1)}, f32[4,16,9,8,128]{4,3,2,1,0:T(8,128)S(1)}) custom-call(s32[2,2,8]{2,1,0:T(2,128)S(1)} %copy-done.2, s32[1]{0:T(128)} %bitcast.depth_ref, f32[4096,128]{1,0:T(8,128)S(1)} %bitcast.23, f32[4096,128]{1,0:T(8,128)S(1)} %bitcast.25, f32[1024,128]{1,0:T(8,128)S(1)} %bitcast.27, ...), custom_call_target="tpu_custom_call" | custom-call | tf_op jit(solution)/shard_map/ends/pallas_call | solution.py:478
  23.0 0.1 collective-permute-start.2
  23.1 1.5 %collective-permute-done.2.got_ref = f32[2,4,16,512]{3,2,1,0:T(8,128)S(1)} collective-permute-done((f32[2,4,16,512]{3,2,1,0:T(8,128)S(1)}, f32[2,4,16,512]{3,2,1,0:T(8,128)S(1)}, u32[]{:S(2)}, u32[]{:S(2)}) %collective-permute-start.2) | collective-permute-done | bytes 262176 | tf_op jit(solution)/shard_map/ppermute | solution.py:403
  24.7 1.7 %collective-permute-start.3 = (f32[4,16,512]{2,1,0:T(8,128)S(1)}, f32[4,16,512]{2,1,0:T(8,128)S(1)}, u32[]{:S(2)}, u32[]{:S(2)}) collective-permute-start(f32[4,16,512]{2,1,0:T(8,128)S(1)} %get-tuple-element.23.refs_0_), channel_id=1, source_target_pairs={{0,2},{1,3},{2,0},{3,1},{4,6},{5,7},{6,4},{7,5},{8,10},{9,11},{10,... | collective-permute-start | bytes 393224 | tf_op jit(solution)/shard_map/ppermute | solution.py:489
  26.3 0.0 collective-permute-done.4.pair_ref
  26.4 0.0 collective-permute-done.5.cross_ref
  26.4 0.4 %edges.2.refs_0_ = f32[2,4,8,256]{3,2,1,0:T(8,128)S(1)} custom-call(s32[1]{0:T(128)} %bitcast.depth_ref, s32[1]{0:T(128)} %bitcast.7.lat_ref, f32[8,16,9,8,128]{4,3,2,1,0:T(8,128)S(1)} %get-tuple-element.19.middle_kept_ref.kept_ref, f32[4,16,9,8,128]{4,3,2,1,0:T(8,128)S(1)} %get-tuple-element.24.ends_ref, ...), custom_call_target="tpu_custom_call" | custom-call | tf_op jit(solution)/shard_map/edges/pallas_call | solution.py:503
  26.7 0.2 collective-permute-start.7
  26.9 0.4 %edges.3.home_ref = f32[2,4,8,256]{3,2,1,0:T(8,128)S(1)} custom-call(s32[1]{0:T(128)} %bitcast.depth_ref, s32[1]{0:T(128)} %bitcast.7.lat_ref, f32[8,16,9,8,128]{4,3,2,1,0:T(8,128)S(1)} %get-tuple-element.19.middle_kept_ref.kept_ref, f32[4,16,9,8,128]{4,3,2,1,0:T(8,128)S(1)} %get-tuple-element.24.ends_ref, ...), custom_call_target="tpu_custom_call" | custom-call | tf_op jit(solution)/shard_map/edges/pallas_call | solution.py:503
  27.2 1.9 %collective-permute-start.6 = (f32[2,4,8,256]{3,2,1,0:T(8,128)S(1)}, f32[2,4,8,256]{3,2,1,0:T(8,128)S(1)}, u32[]{:S(2)}, u32[]{:S(2)}) collective-permute-start(f32[2,4,8,256]{3,2,1,0:T(8,128)S(1)} %edges.3.home_ref), channel_id=1, source_target_pairs={{0,1},{1,0},{2,3},{3,2},{4,5},{5,4},{6,7},{7,6},{8,9},{9,8},{10,11... | collective-permute-start | bytes 196616 | tf_op jit(solution)/shard_map/ppermute | solution.py:403
  29.1 2.2 %collective-permute-done.7.across_ref = f32[2,4,8,256]{3,2,1,0:T(8,128)S(1)} collective-permute-done((f32[2,4,8,256]{3,2,1,0:T(8,128)S(1)}, f32[2,4,8,256]{3,2,1,0:T(8,128)S(1)}, u32[]{:S(2)}, u32[]{:S(2)}) %collective-permute-start.7) | collective-permute-done | bytes 65568 | tf_op jit(solution)/shard_map/ppermute | solution.py:489
  31.3 0.9 %collective-permute-start.8 = (f32[2,4,8,256]{3,2,1,0:T(8,128)S(1)}, f32[2,4,8,256]{3,2,1,0:T(8,128)S(1)}, u32[]{:S(2)}, u32[]{:S(2)}) collective-permute-start(f32[2,4,8,256]{3,2,1,0:T(8,128)S(1)} %collective-permute-done.7.across_ref), channel_id=1, source_target_pairs={{0,1},{1,0},{2,3},{3,2},{4,5},{5,4},{6,7},{7,6},{8,9},{9,8},{10,11... | collective-permute-start | bytes 196616 | tf_op jit(solution)/shard_map/ppermute | solution.py:403
  32.2 0.0 collective-permute-done.6.beside_ref
  32.2 0.0 collective-permute-done.3.got_ref
  32.2 0.9 %collective-permute-done.8.corner_ref = f32[2,4,8,256]{3,2,1,0:T(8,128)S(1)} collective-permute-done((f32[2,4,8,256]{3,2,1,0:T(8,128)S(1)}, f32[2,4,8,256]{3,2,1,0:T(8,128)S(1)}, u32[]{:S(2)}, u32[]{:S(2)}) %collective-permute-start.8) | collective-permute-done | bytes 65568 | tf_op jit(solution)/shard_map/ppermute | solution.py:403
  33.1 0.7 %finish.1 = f32[4,16,512]{2,1,0:T(8,128)} custom-call(s32[1]{0:T(128)} %bitcast.depth_ref, f32[4,16,512]{2,1,0:T(8,128)S(1)} %get-tuple-element.22.own_ref, f32[4,16,512]{2,1,0:T(8,128)S(1)} %collective-permute-done.3.got_ref, f32[2,4,8,256]{3,2,1,0:T(8,128)S(1)} %edges.3.home_ref, f32[2,4,8,256]{3,2,1,0:T(8,128)S(1)} %collective-permute-done.6.beside_ref, ...), custom_call_target="tpu_custom_call" | custom-call | tf_op jit(solution)/shard_map/finish/pallas_call | solution.py:516
  (3 shorter events, 0.0 us)
Async XLA Ops:
  1.1 25.2 %collective-permute-start.4 = (f32[2,4,8,2048]{3,2,1,0:T(8,128)S(1)}, f32[2,4,8,2048]{3,2,1,0:T(8,128)S(1)}, u32[]{:S(2)}, u32[]{:S(2)}) collective-permute-start(f32[2,4,8,2048]{3,2,1,0:T(8,128)S(1)} %take_pair.1.after_ref), channel_id=1, source_target_pairs={{0,4},{4,0},{8,12},{12,8},{16,20},{20,16},{24,28},{28,24},{1,5},{5... | collective-permute-start | bytes 1572872 | tf_op jit(solution)/shard_map/ppermute | solution.py:403
  1.4 10.4 %copy-start.1 = (f32[16,16,2048]{2,1,0:T(8,128)S(1)}, f32[16,16,2048]{2,1,0:T(8,128)}, u32[]{:S(2)}) copy-start(f32[16,16,2048]{2,1,0:T(8,128)} %amp_hbm.3) | copy-start | bytes 6291460
  3.1 8.7 %copy-start = (f32[16,16,2048]{2,1,0:T(8,128)S(1)}, f32[16,16,2048]{2,1,0:T(8,128)}, u32[]{:S(2)}) copy-start(f32[16,16,2048]{2,1,0:T(8,128)} %grade_hbm.3) | copy-start | bytes 6291460
  3.1 8.7 %copy-start.2 = (s32[2,2,8]{2,1,0:T(2,128)S(1)}, s32[2,2,8]{2,1,0:T(2,128)}, u32[]{:S(2)}) copy-start(s32[2,2,8]{2,1,0:T(2,128)} %mask_ref.3) | copy-start | bytes 388
  3.2 8.7 %copy-start.3 = (s32[4,128]{1,0:T(4,128)S(1)}, s32[4,128]{1,0:T(4,128)}, u32[]{:S(2)}) copy-start(s32[4,128]{1,0:T(4,128)} %table_ref.3) | copy-start | bytes 6148
  3.2 23.2 %collective-permute-start.5 = (f32[2,4,8,2048]{3,2,1,0:T(8,128)S(1)}, f32[2,4,8,2048]{3,2,1,0:T(8,128)S(1)}, u32[]{:S(2)}, u32[]{:S(2)}) collective-permute-start(f32[2,4,8,2048]{3,2,1,0:T(8,128)S(1)} %get-tuple-element.17.refs_1_), channel_id=1, source_target_pairs={{4,8},{8,4},{12,16},{16,12},{20,24},{24,20},{5,9},{9,5},{13,17},{1... | collective-permute-start | bytes 1572872 | tf_op jit(solution)/shard_map/ppermute | solution.py:408
  7.5 11.4 %collective-permute-start.1 = (f32[2,2,16,2048]{3,2,1,0:T(8,128)S(1)}, f32[2,2,16,2048]{3,2,1,0:T(8,128)S(1)}, u32[]{:S(2)}, u32[]{:S(2)}) collective-permute-start(f32[2,2,16,2048]{3,2,1,0:T(8,128)S(1)} %pass_on.2.refs_1_), channel_id=1, source_target_pairs={{1,2},{2,1},{5,6},{6,5},{9,10},{10,9},{13,14},{14,13},{17,18},{18,... | collective-permute-start | bytes 1572872 | tf_op jit(solution)/shard_map/ppermute | solution.py:408
  11.7 6.5 %collective-permute-start = (f32[2,2,16,2048]{3,2,1,0:T(8,128)S(1)}, f32[2,2,16,2048]{3,2,1,0:T(8,128)S(1)}, u32[]{:S(2)}, u32[]{:S(2)}) collective-permute-start(f32[2,2,16,2048]{3,2,1,0:T(8,128)S(1)} %pass_on.3), channel_id=1, source_target_pairs={{0,1},{1,0},{2,3},{3,2},{4,5},{5,4},{6,7},{7,6},{8,9},{9,8},{10,11... | collective-permute-start | bytes 1572872 | tf_op jit(solution)/shard_map/ppermute | solution.py:403
  23.0 1.6 %collective-permute-start.2 = (f32[2,4,16,512]{3,2,1,0:T(8,128)S(1)}, f32[2,4,16,512]{3,2,1,0:T(8,128)S(1)}, u32[]{:S(2)}, u32[]{:S(2)}) collective-permute-start(f32[2,4,16,512]{3,2,1,0:T(8,128)S(1)} %get-tuple-element.21), channel_id=1, source_target_pairs={{0,1},{1,0},{2,3},{3,2},{4,5},{5,4},{6,7},{7,6},{8,9},{9,8},{10,11... | collective-permute-start | bytes 786440 | tf_op jit(solution)/shard_map/ppermute | solution.py:403
  24.7 7.5 %collective-permute-start.3 = (f32[4,16,512]{2,1,0:T(8,128)S(1)}, f32[4,16,512]{2,1,0:T(8,128)S(1)}, u32[]{:S(2)}, u32[]{:S(2)}) collective-permute-start(f32[4,16,512]{2,1,0:T(8,128)S(1)} %get-tuple-element.23.refs_0_), channel_id=1, source_target_pairs={{0,2},{1,3},{2,0},{3,1},{4,6},{5,7},{6,4},{7,5},{8,10},{9,11},{10,... | collective-permute-start | bytes 393224 | tf_op jit(solution)/shard_map/ppermute | solution.py:489
  26.7 4.6 %collective-permute-start.7 = (f32[2,4,8,256]{3,2,1,0:T(8,128)S(1)}, f32[2,4,8,256]{3,2,1,0:T(8,128)S(1)}, u32[]{:S(2)}, u32[]{:S(2)}) collective-permute-start(f32[2,4,8,256]{3,2,1,0:T(8,128)S(1)} %edges.2.refs_0_), channel_id=1, source_target_pairs={{0,2},{1,3},{2,0},{3,1},{4,6},{5,7},{6,4},{7,5},{8,10},{9,11},{10,... | collective-permute-start | bytes 196616 | tf_op jit(solution)/shard_map/ppermute | solution.py:489
  27.2 5.0 %collective-permute-start.6 = (f32[2,4,8,256]{3,2,1,0:T(8,128)S(1)}, f32[2,4,8,256]{3,2,1,0:T(8,128)S(1)}, u32[]{:S(2)}, u32[]{:S(2)}) collective-permute-start(f32[2,4,8,256]{3,2,1,0:T(8,128)S(1)} %edges.3.home_ref), channel_id=1, source_target_pairs={{0,1},{1,0},{2,3},{3,2},{4,5},{5,4},{6,7},{7,6},{8,9},{9,8},{10,11... | collective-permute-start | bytes 196616 | tf_op jit(solution)/shard_map/ppermute | solution.py:403
  31.3 1.8 %collective-permute-start.8 = (f32[2,4,8,256]{3,2,1,0:T(8,128)S(1)}, f32[2,4,8,256]{3,2,1,0:T(8,128)S(1)}, u32[]{:S(2)}, u32[]{:S(2)}) collective-permute-start(f32[2,4,8,256]{3,2,1,0:T(8,128)S(1)} %collective-permute-done.7.across_ref), channel_id=1, source_target_pairs={{0,1},{1,0},{2,3},{3,2},{4,5},{5,4},{6,7},{7,6},{8,9},{9,8},{10,11... | collective-permute-start | bytes 196616 | tf_op jit(solution)/shard_map/ppermute | solution.py:403
